TPU v7x, 128 devices: a whole 4x4x4 slice. The times are simulated.
128 devices in a mesh: fsdp: 16 (over z_hi, x, core), tensor: 8 (over z_lo, y).
Axes of the slice: x: 4, y: 4, z: 4 (z_hi: 2, z_lo: 2; z = z_hi * 2 + z_lo), core: 2. Of those that a mesh axis runs over, the one named last changes fastest.
Arguments:
- saved_weight: float32 [7168, 8192], P(('fsdp', 'tensor')), may hold values from -6 to 6
- saved_first: float32 [7168, 8192], P(('fsdp', 'tensor')), may hold values from -3 to 3
- saved_second: float32 [7168, 8192], P(('fsdp', 'tensor')), may hold values from 0.1 to 2
- saved_order: int32 [7168], P(('fsdp', 'tensor')), may hold values from 0 to 55, as said below
- mask: int32 [7168, 8192], P('tensor', 'fsdp'), may hold values 0 or 1
- hidden: bfloat16 [4096, 7168], P('fsdp', 'tensor'), may hold values from -6 to 6
- cotangent: bfloat16 [4096, 8192], P('fsdp'), may hold values from -6 to 6
Outputs:
- output: bfloat16 [4096, 8192], P('fsdp', 'tensor')
- hidden_grad: bfloat16 [4096, 7168], P('fsdp', 'tensor')
- new_weight: float32 [7168, 8192], P('tensor', 'fsdp')
- new_first: float32 [7168, 8192], P('tensor', 'fsdp')
- new_second: float32 [7168, 8192], P('tensor', 'fsdp')
Inputs may be any that keep to these rules, and one draw needn't show every extreme that they name: `saved_order`: each aligned block of 56 entries holds every number of 0 to 55 once.
All inputs are finite; a program needn't handle non-finite values. No bound on the sum of `mask` on one device may be relied on, other than what follows from the above.
Results may differ from a plain program's by a relative error of at most 0.005.
Values may be sent and summed in bfloat16 or wider, within the bound.
No kernel may reach another device: no remote copies, remote signals or barrier semaphores. Data moves between devices by JAX's collectives and lax.ppermute only.
A program may use at most 128 MiB of HBM per device.

v0:
```python
import jax
import jax.numpy as jnp
from jax import lax
from jax.sharding import PartitionSpec as P


R = 7168
STEP = 1000


beta_first = 0.9
beta_second = 0.999
learn_rate = 0.01
decay_rate = 0.1
epsilon = 1e-08


XS = 4
YS = 4
SPREAD = (2, 1, 0, 3)


def fsdp_id(zh, x, core):
    return (zh * XS + x) * 2 + core


def shift_x(value, k):
    pairs = [
        (fsdp_id(zh, x, core), fsdp_id(zh, (x + k) % XS, core))
        for zh in range(2)
        for x in range(XS)
        for core in range(2)
    ]
    return lax.ppermute(value, "fsdp", pairs)


def swap_zh(value):
    return lax.ppermute(value, "fsdp", [(i, i ^ 8) for i in range(16)])


def swap_core(value):
    return lax.ppermute(value, "fsdp", [(i, i ^ 1) for i in range(16)])


def shift_y(value, k):
    pairs = [(zl * YS + y, zl * YS + (y + k) % YS) for zl in range(2) for y in range(YS)]
    return lax.ppermute(value, "tensor", pairs)


def swap_zl_half(value, near):
    pairs = []
    for f in range(16):
        keeper = f // 8 if near else 1 - f // 8
        for y in range(YS):
            pairs.append((f * 8 + (1 - keeper) * YS + y, f * 8 + keeper * YS + y))
    return lax.ppermute(value, ("fsdp", "tensor"), pairs)


def place_output(value, near):
    pairs = []
    for f in range(16):
        zh, x, core = f // 8, (f // 2) % 4, f % 2
        zl = zh if near else 1 - zh
        for y in range(YS):
            there = fsdp_id(zh, (x + SPREAD[(y - x) % 4]) % XS, core)
            pairs.append((f * 8 + zl * YS + y, there * 8 + zl * YS + x))
    return lax.ppermute(value, ("fsdp", "tensor"), pairs)


def stacked(pieces):
    n = pieces[0].shape[0]
    whole = jnp.zeros((n * len(pieces),) + pieces[0].shape[1:], pieces[0].dtype)
    for k, piece in enumerate(pieces):
        whole = lax.dynamic_update_slice_in_dim(whole, piece, k * n, axis=0)
    return whole


def body(saved_weight, saved_first, saved_second, saved_order, mask, hidden, cotangent):
    f32, bf16 = jnp.float32, jnp.bfloat16
    band = saved_order.shape[0]
    toks, rows = hidden.shape
    cols = mask.shape[1]
    f = lax.axis_index("fsdp")
    t = lax.axis_index("tensor")
    zh, x, core = f >> 3, (f >> 1) & 3, f & 1
    zl, y = t >> 2, t & 3
    alpha = R ** (-0.5)

    pick = (saved_order[None, :] == jnp.arange(band, dtype=jnp.int32)[:, None]).astype(bf16)

    def arranged(saved):
        moved = jnp.dot(pick, saved.astype(bf16), preferred_element_type=f32).astype(bf16)
        return moved.reshape(band, 16, cols).transpose(1, 0, 2)

    def to_columns(blocks):
        return lax.all_to_all(blocks, "fsdp", split_axis=0, concat_axis=0, tiled=True)

    def to_rows(blocks):
        n = blocks.shape[1]
        got = lax.all_to_all(blocks, "tensor", split_axis=0, concat_axis=0, tiled=True)
        return got.reshape(8, 2, n, cols).transpose(1, 0, 2, 3).reshape(16, n, cols)

    weight_columns = to_columns(arranged(saved_weight))
    weight = to_rows(weight_columns).reshape(rows, cols)
    masked = weight * mask.astype(bf16)

    pieces = [hidden]
    for k in (1, 2, 3):
        pieces.append(shift_x(hidden, k))
    hidden_all = stacked(pieces)

    def cot_for(k):
        there = (x + k) & 3
        parts = [
            lax.dynamic_slice_in_dim(
                cotangent, fsdp_id(zh ^ zr, there, core ^ cr) * cols, cols, axis=1
            )
            for cr in (0, 1)
            for zr in (0, 1)
        ]
        return jnp.concatenate(parts, axis=1)

    pieces = [cot_for(0)]
    for k in (1, 2, 3):
        pieces.append(shift_x(cot_for(k), k))
    cot_pieces = pieces

    masked_core = swap_core(masked)
    masked_zh = swap_zh(masked)
    masked_far = swap_core(masked_zh)

    def output_half(own, other, near):
        parts = []
        for block in (own, other):
            product = alpha * jnp.dot(hidden_all, block, preferred_element_type=f32)
            parts.append(product.astype(bf16).reshape(XS, toks, cols))

        def chunk_of(yy):
            e = (yy - x) & 3
            there = jnp.where(e == 0, SPREAD[0], jnp.where(e == 2, SPREAD[2], e))
            k = (-there) & 3
            return jnp.concatenate(
                [lax.dynamic_index_in_dim(p, k, axis=0, keepdims=False) for p in parts], axis=1
            )

        got = []
        for k in (1, 2, 3):
            got.append(shift_y(chunk_of((y + k) & 3), k))
        own_chunk = chunk_of(y)
        total = own_chunk.astype(f32)
        for piece in got:
            total = total + piece.astype(f32)
        sent = total.astype(bf16)
        got = swap_zl_half(sent, near)
        total = (total + got.astype(f32)).astype(bf16)
        total = jnp.where(
            core == 0, total, jnp.concatenate([total[:, cols:], total[:, :cols]], axis=1)
        )
        return place_output(total, near)

    out_near = output_half(masked, masked_core, True)
    out_far = output_half(masked_zh, masked_far, False)
    output = jnp.where(zl == zh, out_near, out_far)

    columns = jnp.concatenate([masked, masked_zh, masked_core, masked_far], axis=1)
    cot_all = stacked(cot_pieces)
    back = (
        alpha
        * lax.dot_general(cot_all, columns, (((1,), (1,)), ((), ())), preferred_element_type=f32)
    ).astype(bf16).reshape(XS, toks, rows)
    got = []
    for k in (1, 2, 3):
        got.append(shift_x(back[k], -k))
    hidden_grad = back[0].astype(f32)
    for piece in got:
        hidden_grad = hidden_grad + piece.astype(f32)
    hidden_grad = hidden_grad.astype(bf16)

    def product(block):
        return (
            alpha
            * lax.dot_general(
                hidden_all, block, (((0,), (0,)), ((), ())), preferred_element_type=f32
            )
        ).astype(bf16)

    away = product(cot_all[:, 2 * cols :])
    stay = product(cot_all[:, : 2 * cols])
    from_core = swap_core(away)
    far = (stay[:, cols:].astype(f32) + from_core[:, cols:].astype(f32)).astype(bf16)
    from_zh = swap_zh(far)
    summed = stay[:, :cols].astype(f32) + from_core[:, :cols].astype(f32) + from_zh.astype(f32)

    moment_blocks = jnp.concatenate(
        [arranged(saved_first), arranged(saved_second)], axis=1
    )
    moments = to_columns(moment_blocks)
    moments = to_rows(moments)
    first = moments[:, :band].reshape(rows, cols).astype(f32)
    second = moments[:, band:].reshape(rows, cols).astype(f32)
    weight = weight.astype(f32)

    keep = mask.astype(f32)
    grad = keep * summed
    new_first = beta_first * first + (1.0 - beta_first) * grad
    new_second = beta_second * second + (1.0 - beta_second) * grad * grad
    corr_first = 1.0 - beta_first ** (STEP + 1)
    corr_second = 1.0 - beta_second ** (STEP + 1)
    update = new_first / corr_first / (jnp.sqrt(new_second / corr_second) + epsilon)
    new_weight = keep * (weight - learn_rate * (update + decay_rate * weight))
    return (output, hidden_grad, new_weight, new_first, new_second)


def solution(mesh):
    return jax.shard_map(
        body,
        mesh=mesh,
        in_specs=(
            P(("fsdp", "tensor"), None),
            P(("fsdp", "tensor"), None),
            P(("fsdp", "tensor"), None),
            P(("fsdp", "tensor")),
            P("tensor", "fsdp"),
            P("fsdp", "tensor"),
            P("fsdp", None),
        ),
        out_specs=(
            P("fsdp", "tensor"),
            P("fsdp", "tensor"),
            P("tensor", "fsdp"),
            P("tensor", "fsdp"),
            P("tensor", "fsdp"),
        ),
        check_vma=False,
    )
```

profile of v0, /device:TPU:1, one launch (start us, length us, event | category | flops | bytes accessed | tf_op | source)
XLA Modules:
  0.0 240.8 jit_solution(9024570412884978188)
XLA Ops:
  9.2 6.7 %all-to-all-start = ((bf16[16,56,512]{2,1,0:T(8,128)(2,1)}), bf16[16,56,512]{2,1,0:T(8,128)(2,1)}, u32[]{:S(2)}, u32[]{:S(2)}) async-start(bf16[16,56,512]{2,1,0:T(8,128)(2,1)} %bitcast.79), calls=%async_computation | async-start | bytes 1835008 | tf_op jit(solution)/shard_map/all_to_all | solution.py:96
  24.9 7.9 %fusion.6 = bf16[1024,2048]{1,0:T(8,128)(2,1)} fusion(bf16[256,512]{1,0:T(8,128)(2,1)S(1)} %get-tuple-element.18, bf16[256,512]{1,0:T(8,128)(2,1)S(1)} %get-tuple-element.19, bf16[256,512]{1,0:T(8,128)(2,1)S(1)} %get-tuple-element.20, bf16[256,512]{1,0:T(8,128)(2,1)S(1)} %get-tuple-element.21), kind=kLoop, calls=%fused_computation.10 | loop fusion | flops 27262976 | bytes 5242880 | tf_op jit(solution)/shard_map/concatenate | solution.py:121
  39.5 4.8 %all-to-all-start.1 = ((bf16[16,56,512]{2,1,0:T(8,128)(2,1)}), bf16[16,56,512]{2,1,0:T(8,128)(2,1)S(1)}, u32[]{:S(2)}, u32[]{:S(2)}) async-start(bf16[16,56,512]{2,1,0:T(8,128)(2,1)} %all-to-all-done), calls=%async_computation.1 | async-start | bytes 1835008 | tf_op jit(solution)/shard_map/all_to_all | solution.py:100
  46.5 13.2 %collective-permute-done.16 = bf16[256,2048]{1,0:T(8,128)(2,1)} collective-permute-done((bf16[256,2048]{1,0:T(8,128)(2,1)}, bf16[256,2048]{1,0:T(8,128)(2,1)}, u32[]{:S(2)}, u32[]{:S(2)}) %collective-permute-start.16) | collective-permute-done | bytes 1048608 | tf_op jit(solution)/shard_map/ppermute | solution.py:34
  62.0 18.1 %collective-permute-done.17 = bf16[256,2048]{1,0:T(8,128)(2,1)} collective-permute-done((bf16[256,2048]{1,0:T(8,128)(2,1)}, bf16[256,2048]{1,0:T(8,128)(2,1)}, u32[]{:S(2)}, u32[]{:S(2)}) %collective-permute-start.17) | collective-permute-done | bytes 1048608 | tf_op jit(solution)/shard_map/ppermute | solution.py:34
  83.3 7.0 %all-to-all-start.2 = ((bf16[16,112,512]{2,1,0:T(8,128)(2,1)}), bf16[16,112,512]{2,1,0:T(8,128)(2,1)}, u32[]{:S(2)}, u32[]{:S(2)}) async-start(bf16[16,112,512]{2,1,0:T(8,128)(2,1)} %pad_maximum_fusion), calls=%async_computation.2 | async-start | bytes 3670016 | tf_op jit(solution)/shard_map/all_to_all | solution.py:96
  95.5 5.0 %multiply_convert_fusion = bf16[896,1024]{1,0:T(8,128)(2,1)} fusion(bf16[1024,896]{1,0:T(8,128)(2,1)} %copy-done.13, bf16[1024,2048]{1,0:T(8,128)(2,1)S(1)} %copy-done.1), kind=kOutput, calls=%fused_computation.19 | convolution fusion | flops 1880883200 | bytes 5767168 | tf_op jit(solution)/shard_map/dot_general | solution.py:182
  100.9 3.4 %multiply_convert_fusion.1 = bf16[896,1024]{1,0:T(8,128)(2,1)} fusion(bf16[1024,896]{1,0:T(8,128)(2,1)S(1)} %copy-done.14, bf16[1024,2048]{1,0:T(8,128)(2,1)S(1)} %copy-done.1), kind=kOutput, calls=%fused_computation.20 | convolution fusion | flops 1880883200 | bytes 5767168 | tf_op jit(solution)/shard_map/dot_general | solution.py:182
  107.1 3.4 %multiply_convert_fusion.6 = bf16[1024,512]{1,0:T(8,128)(2,1)} fusion(bf16[1024,896]{1,0:T(8,128)(2,1)S(1)} %copy-done.14, bf16[896,512]{1,0:T(8,128)(2,1)} %bitcast_multiply_fusion), kind=kOutput, calls=%fused_computation.32 | convolution fusion | flops 940572672 | bytes 3801088 | tf_op jit(solution)/shard_map/dot_general | solution.py:135
  110.5 5.6 %all-to-all-done.2 = bf16[16,112,512]{2,1,0:T(8,128)(2,1)} async-done(((bf16[16,112,512]{2,1,0:T(8,128)(2,1)}), bf16[16,112,512]{2,1,0:T(8,128)(2,1)}, u32[]{:S(2)}, u32[]{:S(2)}) %all-to-all-start.2) | async-done | bytes 1835040 | tf_op jit(solution)/shard_map/all_to_all | solution.py:96
  116.1 4.6 %all-to-all-start.3 = ((bf16[16,112,512]{2,1,0:T(8,128)(2,1)}), bf16[16,112,512]{2,1,0:T(8,128)(2,1)}, u32[]{:S(2)}, u32[]{:S(2)}) async-start(bf16[16,112,512]{2,1,0:T(8,128)(2,1)} %all-to-all-done.2), calls=%async_computation.3 | async-start | bytes 3670016 | tf_op jit(solution)/shard_map/all_to_all | solution.py:100
  120.8 3.1 %multiply_convert_fusion.5 = bf16[1024,512]{1,0:T(8,128)(2,1)S(1)} fusion(bf16[1024,896]{1,0:T(8,128)(2,1)} %copy-done.13, bf16[896,512]{1,0:T(8,128)(2,1)} %collective-permute-done.3), kind=kOutput, calls=%fused_computation.31 | convolution fusion | flops 940572672 | bytes 3801088 | tf_op jit(solution)/shard_map/dot_general | solution.py:135
  128.3 20.7 %collective-permute-done.9 = bf16[896,512]{1,0:T(8,128)(2,1)} collective-permute-done((bf16[896,512]{1,0:T(8,128)(2,1)}, bf16[896,512]{1,0:T(8,128)(2,1)}, u32[]{:S(2)}, u32[]{:S(2)}) %collective-permute-start.9) | collective-permute-done | bytes 917536 | tf_op jit(solution)/shard_map/ppermute | solution.py:38
  149.4 3.4 %multiply_convert_fusion.4 = bf16[1024,512]{1,0:T(8,128)(2,1)} fusion(bf16[1024,896]{1,0:T(8,128)(2,1)S(1)} %copy-done.15, bf16[896,512]{1,0:T(8,128)(2,1)} %collective-permute-done.9), kind=kOutput, calls=%fused_computation.30 | convolution fusion | flops 940572672 | bytes 3801088 | tf_op jit(solution)/shard_map/dot_general | solution.py:135
  155.6 11.2 %collective-permute-done.4 = bf16[256,1024]{1,0:T(8,128)(2,1)S(1)} collective-permute-done((bf16[256,1024]{1,0:T(8,128)(2,1)S(1)}, bf16[256,1024]{1,0:T(8,128)(2,1)S(1)}, u32[]{:S(2)}, u32[]{:S(2)}) %collective-permute-start.4) | collective-permute-done | bytes 524320 | tf_op jit(solution)/shard_map/ppermute | solution.py:47
  177.6 6.5 %multiply_convert_fusion.2 = bf16[1024,896]{1,0:T(8,128)(2,1)S(1)} fusion(bf16[1024,2048]{1,0:T(8,128)(2,1)S(1)} %copy-done.2, bf16[896,512]{1,0:T(8,128)(2,1)} %collective-permute-done.10, bf16[896,512]{1,0:T(8,128)(2,1)} %collective-permute-done.3, bf16[896,512]{1,0:T(8,128)(2,1)} %collective-permute-done.9, bf16[896,512]{1,0:T(8,128)(2,1)} %bitcast_multiply_fusion), kind=kOutput, calls=%fused_computation.21 | convolution fusion | flops 3774611456 | bytes 9699328 | tf_op jit(solution)/shard_map/dot_general | solution.py:169
  184.3 3.7 %collective-permute-done.13 = bf16[256,1024]{1,0:T(8,128)(2,1)S(1)} collective-permute-done((bf16[256,1024]{1,0:T(8,128)(2,1)S(1)}, bf16[256,1024]{1,0:T(8,128)(2,1)S(1)}, u32[]{:S(2)}, u32[]{:S(2)}) %collective-permute-start.13) | collective-permute-done | bytes 524320 | tf_op jit(solution)/shard_map/ppermute | solution.py:47
  189.2 16.2 %collective-permute-start.20 = (bf16[256,896]{1,0:T(8,128)(2,1)S(1)}, bf16[256,896]{1,0:T(8,128)(2,1)S(1)}, u32[]{:S(2)}, u32[]{:S(2)}) collective-permute-start(bf16[256,896]{1,0:T(8,128)(2,1)S(1)} %get-tuple-element.28), channel_id=1, source_target_pairs={{0,32},{8,40},{16,48},{24,56},{32,0},{40,8},{48,16},{56,24},{64,96... | collective-permute-start | bytes 1376264 | tf_op jit(solution)/shard_map/ppermute | solution.py:34
  205.4 3.7 %collective-permute-start.19 = (bf16[256,896]{1,0:T(8,128)(2,1)S(1)}, bf16[256,896]{1,0:T(8,128)(2,1)S(1)}, u32[]{:S(2)}, u32[]{:S(2)}) collective-permute-start(bf16[256,896]{1,0:T(8,128)(2,1)S(1)} %get-tuple-element.26), channel_id=1, source_target_pairs={{0,48},{8,56},{16,0},{24,8},{32,16},{40,24},{48,32},{56,40},{64,11... | collective-permute-start | bytes 1376264 | tf_op jit(solution)/shard_map/ppermute | solution.py:34
  209.4 4.8 %collective-permute-start.14 = (bf16[256,1024]{1,0:T(8,128)(2,1)S(1)}, bf16[256,1024]{1,0:T(8,128)(2,1)S(1)}, u32[]{:S(2)}, u32[]{:S(2)}) collective-permute-start(bf16[256,1024]{1,0:T(8,128)(2,1)S(1)} %fusion.33), channel_id=1, source_target_pairs={{0,4},{1,5},{2,6},{3,7},{8,12},{9,13},{10,14},{11,15},{16,20},{17,... | collective-permute-start | bytes 1572872 | tf_op jit(solution)/shard_map/ppermute | solution.py:56
  216.0 8.7 %collective-permute-done.14 = bf16[256,1024]{1,0:T(8,128)(2,1)S(1)} collective-permute-done((bf16[256,1024]{1,0:T(8,128)(2,1)S(1)}, bf16[256,1024]{1,0:T(8,128)(2,1)S(1)}, u32[]{:S(2)}, u32[]{:S(2)}) %collective-permute-start.14) | collective-permute-done | bytes 524320 | tf_op jit(solution)/shard_map/ppermute | solution.py:56
  224.7 2.9 %collective-permute-start.8 = (bf16[256,1024]{1,0:T(8,128)(2,1)S(1)}, bf16[256,1024]{1,0:T(8,128)(2,1)S(1)}, u32[]{:S(2)}, u32[]{:S(2)}) collective-permute-start(bf16[256,1024]{1,0:T(8,128)(2,1)S(1)} %maximum_select_fusion), channel_id=1, source_target_pairs={{0,32},{1,16},{2,0},{3,48},{8,40},{9,24},{10,8},{11,56},{16,1},{17... | collective-permute-start | bytes 1572872 | tf_op jit(solution)/shard_map/ppermute | solution.py:67
  229.6 5.2 %fusion.23 = (f32[896,512]{1,0:T(8,128)}, f32[896,512]{1,0:T(8,128)}, f32[896,512]{1,0:T(8,128)}) fusion(s32[896,512]{1,0:T(8,128)S(1)} %copy-done, bf16[8,2,56,512]{3,2,0,1:T(8,128)(2,1)S(1)} %copy.15, bf16[896,512]{1,0:T(8,128)(2,1)} %collective-permute-done.23, bf16[896,1024]{1,0:T(8,128)(2,1)} %collective-permute-done.22, ...), kind=kLoop, calls=%fused_computation.35 | loop fusion | flops 9633792 | bytes 14680064 | tf_op jit(solution)/shard_map/mul | solution.py:210
  235.8 4.1 %collective-permute-done.8 = bf16[256,1024]{1,0:T(8,128)(2,1)S(1)} collective-permute-done((bf16[256,1024]{1,0:T(8,128)(2,1)S(1)}, bf16[256,1024]{1,0:T(8,128)(2,1)S(1)}, u32[]{:S(2)}, u32[]{:S(2)}) %collective-permute-start.8) | collective-permute-done | bytes 524320 | tf_op jit(solution)/shard_map/ppermute | solution.py:67
  (132 shorter events, 65.6 us)
Async XLA Ops:
  0.6 33.7 %collective-permute-start = (bf16[256,896]{1,0:T(8,128)(2,1)}, bf16[256,896]{1,0:T(8,128)(2,1)S(1)}, u32[]{:S(2)}, u32[]{:S(2)}) collective-permute-start(bf16[256,896]{1,0:T(8,128)(2,1)} %param.12), channel_id=1, source_target_pairs={{0,16},{8,24},{16,32},{24,40},{32,48},{40,56},{48,0},{56,8},{64,80... | collective-permute-start | bytes 1376264 | tf_op jit(solution)/shard_map/ppermute | solution.py:34
  2.7 41.6 %collective-permute-start.1 = (bf16[256,896]{1,0:T(8,128)(2,1)}, bf16[256,896]{1,0:T(8,128)(2,1)}, u32[]{:S(2)}, u32[]{:S(2)}) collective-permute-start(bf16[256,896]{1,0:T(8,128)(2,1)} %param.12), channel_id=1, source_target_pairs={{0,32},{8,40},{16,48},{24,56},{32,0},{40,8},{48,16},{56,24},{64,96... | collective-permute-start | bytes 1376264 | tf_op jit(solution)/shard_map/ppermute | solution.py:34
  5.2 40.2 %collective-permute-start.2 = (bf16[256,896]{1,0:T(8,128)(2,1)}, bf16[256,896]{1,0:T(8,128)(2,1)}, u32[]{:S(2)}, u32[]{:S(2)}) collective-permute-start(bf16[256,896]{1,0:T(8,128)(2,1)} %param.12), channel_id=1, source_target_pairs={{0,48},{8,56},{16,0},{24,8},{32,16},{40,24},{48,32},{56,40},{64,11... | collective-permute-start | bytes 1376264 | tf_op jit(solution)/shard_map/ppermute | solution.py:34
  9.2 30.3 %all-to-all-start = ((bf16[16,56,512]{2,1,0:T(8,128)(2,1)}), bf16[16,56,512]{2,1,0:T(8,128)(2,1)}, u32[]{:S(2)}, u32[]{:S(2)}) async-start(bf16[16,56,512]{2,1,0:T(8,128)(2,1)} %bitcast.79), calls=%async_computation | async-start | bytes 1835008 | tf_op jit(solution)/shard_map/all_to_all | solution.py:96
  19.7 40.0 %collective-permute-start.16 = (bf16[256,2048]{1,0:T(8,128)(2,1)}, bf16[256,2048]{1,0:T(8,128)(2,1)}, u32[]{:S(2)}, u32[]{:S(2)}) collective-permute-start(bf16[256,2048]{1,0:T(8,128)(2,1)} %pad_maximum_fusion.1), channel_id=1, source_target_pairs={{0,16},{8,24},{16,32},{24,40},{32,48},{40,56},{48,0},{56,8},{64,80... | collective-permute-start | bytes 3145736 | tf_op jit(solution)/shard_map/ppermute | solution.py:34
  22.1 58.0 %collective-permute-start.17 = (bf16[256,2048]{1,0:T(8,128)(2,1)}, bf16[256,2048]{1,0:T(8,128)(2,1)}, u32[]{:S(2)}, u32[]{:S(2)}) collective-permute-start(bf16[256,2048]{1,0:T(8,128)(2,1)} %pad_maximum_fusion.2), channel_id=1, source_target_pairs={{0,32},{8,40},{16,48},{24,56},{32,0},{40,8},{48,16},{56,24},{64,96... | collective-permute-start | bytes 3145736 | tf_op jit(solution)/shard_map/ppermute | solution.py:34
  34.3 56.0 %collective-permute-start.18 = (bf16[256,2048]{1,0:T(8,128)(2,1)}, bf16[256,2048]{1,0:T(8,128)(2,1)}, u32[]{:S(2)}, u32[]{:S(2)}) collective-permute-start(bf16[256,2048]{1,0:T(8,128)(2,1)} %pad_maximum_fusion.3), channel_id=1, source_target_pairs={{0,48},{8,56},{16,0},{24,8},{32,16},{40,24},{48,32},{56,40},{64,11... | collective-permute-start | bytes 3145736 | tf_op jit(solution)/shard_map/ppermute | solution.py:34
  39.5 42.9 %all-to-all-start.1 = ((bf16[16,56,512]{2,1,0:T(8,128)(2,1)}), bf16[16,56,512]{2,1,0:T(8,128)(2,1)S(1)}, u32[]{:S(2)}, u32[]{:S(2)}) async-start(bf16[16,56,512]{2,1,0:T(8,128)(2,1)} %all-to-all-done), calls=%async_computation.1 | async-start | bytes 1835008 | tf_op jit(solution)/shard_map/all_to_all | solution.py:100
  83.3 32.8 %all-to-all-start.2 = ((bf16[16,112,512]{2,1,0:T(8,128)(2,1)}), bf16[16,112,512]{2,1,0:T(8,128)(2,1)}, u32[]{:S(2)}, u32[]{:S(2)}) async-start(bf16[16,112,512]{2,1,0:T(8,128)(2,1)} %pad_maximum_fusion), calls=%async_computation.2 | async-start | bytes 3670016 | tf_op jit(solution)/shard_map/all_to_all | solution.py:96
  95.4 25.4 %collective-permute-start.3 = (bf16[896,512]{1,0:T(8,128)(2,1)}, bf16[896,512]{1,0:T(8,128)(2,1)}, u32[]{:S(2)}, u32[]{:S(2)}) collective-permute-start(bf16[896,512]{1,0:T(8,128)(2,1)} %bitcast_multiply_fusion), channel_id=1, source_target_pairs={{0,8},{8,0},{16,24},{24,16},{32,40},{40,32},{48,56},{56,48},{64,72... | collective-permute-start | bytes 2752520 | tf_op jit(solution)/shard_map/ppermute | solution.py:42
  100.5 52.3 %collective-permute-start.22 = (bf16[896,1024]{1,0:T(8,128)(2,1)}, bf16[896,1024]{1,0:T(8,128)(2,1)}, u32[]{:S(2)}, u32[]{:S(2)}) collective-permute-start(bf16[896,1024]{1,0:T(8,128)(2,1)} %multiply_convert_fusion), channel_id=1, source_target_pairs={{0,8},{8,0},{16,24},{24,16},{32,40},{40,32},{48,56},{56,48},{64,72... | collective-permute-start | bytes 5505032 | tf_op jit(solution)/shard_map/ppermute | solution.py:42
  104.3 44.7 %collective-permute-start.9 = (bf16[896,512]{1,0:T(8,128)(2,1)}, bf16[896,512]{1,0:T(8,128)(2,1)}, u32[]{:S(2)}, u32[]{:S(2)}) collective-permute-start(bf16[896,512]{1,0:T(8,128)(2,1)} %bitcast_multiply_fusion), channel_id=1, source_target_pairs={{0,64},{8,72},{16,80},{24,88},{32,96},{40,104},{48,112},{56,120},{... | collective-permute-start | bytes 2752520 | tf_op jit(solution)/shard_map/ppermute | solution.py:38
  116.1 53.1 %all-to-all-start.3 = ((bf16[16,112,512]{2,1,0:T(8,128)(2,1)}), bf16[16,112,512]{2,1,0:T(8,128)(2,1)}, u32[]{:S(2)}, u32[]{:S(2)}) async-start(bf16[16,112,512]{2,1,0:T(8,128)(2,1)} %all-to-all-done.2), calls=%async_computation.3 | async-start | bytes 3670016 | tf_op jit(solution)/shard_map/all_to_all | solution.py:100
  124.1 31.4 %collective-permute-start.6 = (bf16[256,1024]{1,0:T(8,128)(2,1)S(1)}, bf16[256,1024]{1,0:T(8,128)(2,1)S(1)}, u32[]{:S(2)}, u32[]{:S(2)}) collective-permute-start(bf16[256,1024]{1,0:T(8,128)(2,1)S(1)} %pad_maximum_fusion.6), channel_id=1, source_target_pairs={{0,3},{1,0},{2,1},{3,2},{4,7},{5,4},{6,5},{7,6},{8,11},{9,8},{10,9... | collective-permute-start | bytes 1572872 | tf_op jit(solution)/shard_map/ppermute | solution.py:47
  126.9 28.6 %collective-permute-start.5 = (bf16[256,1024]{1,0:T(8,128)(2,1)S(1)}, bf16[256,1024]{1,0:T(8,128)(2,1)S(1)}, u32[]{:S(2)}, u32[]{:S(2)}) collective-permute-start(bf16[256,1024]{1,0:T(8,128)(2,1)S(1)} %pad_maximum_fusion.5), channel_id=1, source_target_pairs={{0,2},{1,3},{2,0},{3,1},{4,6},{5,7},{6,4},{7,5},{8,10},{9,11},{10,... | collective-permute-start | bytes 1572872 | tf_op jit(solution)/shard_map/ppermute | solution.py:47
  127.6 39.2 %collective-permute-start.4 = (bf16[256,1024]{1,0:T(8,128)(2,1)S(1)}, bf16[256,1024]{1,0:T(8,128)(2,1)S(1)}, u32[]{:S(2)}, u32[]{:S(2)}) collective-permute-start(bf16[256,1024]{1,0:T(8,128)(2,1)S(1)} %pad_maximum_fusion.4), channel_id=1, source_target_pairs={{0,1},{1,2},{2,3},{3,0},{4,5},{5,6},{6,7},{7,4},{8,9},{9,10},{10,1... | collective-permute-start | bytes 1572872 | tf_op jit(solution)/shard_map/ppermute | solution.py:47
  149.0 22.4 %collective-permute-start.10 = (bf16[896,512]{1,0:T(8,128)(2,1)}, bf16[896,512]{1,0:T(8,128)(2,1)}, u32[]{:S(2)}, u32[]{:S(2)}) collective-permute-start(bf16[896,512]{1,0:T(8,128)(2,1)} %collective-permute-done.9), channel_id=1, source_target_pairs={{0,8},{8,0},{16,24},{24,16},{32,40},{40,32},{48,56},{56,48},{64,72... | collective-permute-start | bytes 2752520 | tf_op jit(solution)/shard_map/ppermute | solution.py:42
  155.3 73.0 %collective-permute-start.23 = (bf16[896,512]{1,0:T(8,128)(2,1)}, bf16[896,512]{1,0:T(8,128)(2,1)}, u32[]{:S(2)}, u32[]{:S(2)}) collective-permute-start(bf16[896,512]{1,0:T(8,128)(2,1)} %add_convert_fusion), channel_id=1, source_target_pairs={{0,64},{8,72},{16,80},{24,88},{32,96},{40,104},{48,112},{56,120},{... | collective-permute-start | bytes 2752520 | tf_op jit(solution)/shard_map/ppermute | solution.py:38
  167.9 41.5 %collective-permute-start.7 = (bf16[256,1024]{1,0:T(8,128)(2,1)}, bf16[256,1024]{1,0:T(8,128)(2,1)}, u32[]{:S(2)}, u32[]{:S(2)}) collective-permute-start(bf16[256,1024]{1,0:T(8,128)(2,1)} %fusion.32), channel_id=1, source_target_pairs={{4,0},{5,1},{6,2},{7,3},{12,8},{13,9},{14,10},{15,11},{20,16},{21,... | collective-permute-start | bytes 1572872 | tf_op jit(solution)/shard_map/ppermute | solution.py:56
  176.5 28.9 %collective-permute-start.11 = (bf16[256,1024]{1,0:T(8,128)(2,1)S(1)}, bf16[256,1024]{1,0:T(8,128)(2,1)S(1)}, u32[]{:S(2)}, u32[]{:S(2)}) collective-permute-start(bf16[256,1024]{1,0:T(8,128)(2,1)S(1)} %pad_maximum_fusion.7), channel_id=1, source_target_pairs={{0,1},{1,2},{2,3},{3,0},{4,5},{5,6},{6,7},{7,4},{8,9},{9,10},{10,1... | collective-permute-start | bytes 1572872 | tf_op jit(solution)/shard_map/ppermute | solution.py:47
  188.0 46.8 %collective-permute-start.21 = (bf16[256,896]{1,0:T(8,128)(2,1)S(1)}, bf16[256,896]{1,0:T(8,128)(2,1)S(1)}, u32[]{:S(2)}, u32[]{:S(2)}) collective-permute-start(bf16[256,896]{1,0:T(8,128)(2,1)S(1)} %get-tuple-element.27), channel_id=1, source_target_pairs={{0,16},{8,24},{16,32},{24,40},{32,48},{40,56},{48,0},{56,8},{64,80... | collective-permute-start | bytes 1376264 | tf_op jit(solution)/shard_map/ppermute | solution.py:34
  189.2 45.6 %collective-permute-start.20 = (bf16[256,896]{1,0:T(8,128)(2,1)S(1)}, bf16[256,896]{1,0:T(8,128)(2,1)S(1)}, u32[]{:S(2)}, u32[]{:S(2)}) collective-permute-start(bf16[256,896]{1,0:T(8,128)(2,1)S(1)} %get-tuple-element.28), channel_id=1, source_target_pairs={{0,32},{8,40},{16,48},{24,56},{32,0},{40,8},{48,16},{56,24},{64,96... | collective-permute-start | bytes 1376264 | tf_op jit(solution)/shard_map/ppermute | solution.py:34
  205.4 29.4 %collective-permute-start.19 = (bf16[256,896]{1,0:T(8,128)(2,1)S(1)}, bf16[256,896]{1,0:T(8,128)(2,1)S(1)}, u32[]{:S(2)}, u32[]{:S(2)}) collective-permute-start(bf16[256,896]{1,0:T(8,128)(2,1)S(1)} %get-tuple-element.26), channel_id=1, source_target_pairs={{0,48},{8,56},{16,0},{24,8},{32,16},{40,24},{48,32},{56,40},{64,11... | collective-permute-start | bytes 1376264 | tf_op jit(solution)/shard_map/ppermute | solution.py:34
  209.4 15.3 %collective-permute-start.14 = (bf16[256,1024]{1,0:T(8,128)(2,1)S(1)}, bf16[256,1024]{1,0:T(8,128)(2,1)S(1)}, u32[]{:S(2)}, u32[]{:S(2)}) collective-permute-start(bf16[256,1024]{1,0:T(8,128)(2,1)S(1)} %fusion.33), channel_id=1, source_target_pairs={{0,4},{1,5},{2,6},{3,7},{8,12},{9,13},{10,14},{11,15},{16,20},{17,... | collective-permute-start | bytes 1572872 | tf_op jit(solution)/shard_map/ppermute | solution.py:56
  (29 other events, 312.6 us)
where the time goes:
time: 245 us; the launch traced here: 241 us
  waiting for transfers between devices  86.1 us (35%)
  starting transfers between devices  74.7 us (30%)
  matrix products  29.9 us (12%)
  other arithmetic  27.9 us (11%)
  local copies, waits for them, and re-layouts  21.1 us (9%)
    ppermute x9, waiting for transfers between devices, shift_x(): return lax.ppermute(value, 'fsdp', pairs)  31.3 us
    ppermute x9, starting transfers between devices, shift_x(): return lax.ppermute(value, 'fsdp', pairs)  31.1 us
    ppermute x2, waiting for transfers between devices, swap_zh(): return lax.ppermute(value, 'fsdp', [(i, i ^ 8) for i in range(16)])  20.7 us
    ppermute x6, waiting for transfers between devices, shift_y(): return lax.ppermute(value, 'tensor', pairs)  15.5 us
    all_to_all x2, starting transfers between devices, to_columns(): lax.all_to_all(blocks, 'fsdp', split_axis=0, concat_axis=0, tiled=True)  13.7 us
    dot_general x4, matrix products, output_half(): product = alpha * jnp.dot(hidden_all, block, preferred_element_type=f32)  12.3 us
    concatenate x4, other arithmetic, cot_for(): return jnp.concatenate(parts, axis=1)  11.2 us
    dynamic_update_slice x7, local copies, waits for them, and re-layouts, stacked(): whole = lax.dynamic_update_slice_in_dim(whole, piece, k * n, axis=0)  10.6 us
  transfers between devices with their start and end apart: 28, of which 10 were waited for; matrix products, arithmetic and copies ran while one was open for 31% of the time, Pallas kernels for 0%

commit v1 on v0

--- a/solution.py
+++ b/solution.py
@@ -1,6 +1,8 @@
 import jax
 import jax.numpy as jnp
 from jax import lax
+from jax.experimental import pallas as pl
+from jax.experimental.pallas import tpu as pltpu
 from jax.sharding import PartitionSpec as P
 
 
@@ -17,6 +19,7 @@
 
 XS = 4
 YS = 4
+TILE = 512
 SPREAD = (2, 1, 0, 3)
 
 
@@ -67,24 +70,141 @@
     return lax.ppermute(value, ("fsdp", "tensor"), pairs)
 
 
-def stacked(pieces):
-    n = pieces[0].shape[0]
-    whole = jnp.zeros((n * len(pieces),) + pieces[0].shape[1:], pieces[0].dtype)
-    for k, piece in enumerate(pieces):
-        whole = lax.dynamic_update_slice_in_dim(whole, piece, k * n, axis=0)
-    return whole
+VMEM = pl.BlockSpec(memory_space=pltpu.VMEM)
+SMEM = pl.BlockSpec(memory_space=pltpu.SMEM)
+
+
+def forward_kernel(order, h0, h1, h2, h3, own, other, o0, o1, o2, o3, h):
+    alpha = R ** (-0.5)
+    cols = own.shape[1]
+    for k, piece in enumerate((h0, h1, h2, h3)):
+        h[k] = piece[...]
+    for j, out in enumerate((o0, o1, o2, o3)):
+        block_of = h[order[j]]
+        for i, block in enumerate((own, other)):
+            product = jnp.dot(block_of, block[...], preferred_element_type=jnp.float32)
+            out[:, i * cols : (i + 1) * cols] = (alpha * product).astype(jnp.bfloat16)
+
+
+def forward(order, pieces, own, other):
+    (toks, depth), width = pieces[0].shape, 2 * own.shape[1]
+    return pl.pallas_call(
+        forward_kernel,
+        in_specs=[SMEM] + [VMEM] * (XS + 2),
+        out_specs=[VMEM] * XS,
+        out_shape=[jax.ShapeDtypeStruct((toks, width), jnp.bfloat16)] * XS,
+        scratch_shapes=[pltpu.VMEM((XS, toks, depth), jnp.bfloat16)],
+        cost_estimate=pl.CostEstimate(
+            flops=2 * XS * toks * depth * width,
+            bytes_accessed=2 * (XS * toks * depth + depth * width + XS * toks * width),
+            transcendentals=0,
+        ),
+        name="forward",
+    )(order, *pieces, own, other)
+
+
+def turned_product(h_turned, c_refs, lo, hi):
+    columns = jnp.concatenate([c[:, lo:hi] for c in c_refs], axis=0)
+    product = jnp.dot(h_turned[...], columns, preferred_element_type=jnp.float32)
+    return (R ** (-0.5) * product).astype(jnp.bfloat16)
+
+
+def away_kernel(h0, h1, h2, h3, c0, c1, c2, c3, out, h_turned):
+    toks = h0.shape[0]
+    for k, piece in enumerate((h0, h1, h2, h3)):
+        h_turned[:, k * toks : (k + 1) * toks] = piece[...].T
+    half = out.shape[1]
+    for lo in range(0, half, TILE):
+        out[:, lo : lo + TILE] = turned_product(
+            h_turned, (c0, c1, c2, c3), half + lo, half + lo + TILE
+        )
+
+
+def stay_kernel(h_turned, c0, c1, c2, c3, out):
+    for lo in range(0, out.shape[1], TILE):
+        out[:, lo : lo + TILE] = turned_product(h_turned, (c0, c1, c2, c3), lo, lo + TILE)
+
+
+def gradient_cost(pieces, cots):
+    toks, depth = pieces[0].shape
+    half = cots[0].shape[1] // 2
+    return pl.CostEstimate(
+        flops=2 * XS * toks * depth * half,
+        bytes_accessed=2 * (XS * toks * (depth + half) + depth * half),
+        transcendentals=0,
+    )
+
+
+def gradient_away(pieces, cots):
+    toks, depth = pieces[0].shape
+    half = cots[0].shape[1] // 2
+    return pl.pallas_call(
+        away_kernel,
+        in_specs=[VMEM] * (2 * XS),
+        out_specs=[VMEM] * 2,
+        out_shape=[
+            jax.ShapeDtypeStruct((depth, half), jnp.bfloat16),
+            jax.ShapeDtypeStruct((depth, XS * toks), jnp.bfloat16),
+        ],
+        cost_estimate=gradient_cost(pieces, cots),
+        name="away",
+    )(*pieces, *cots)
+
+
+def gradient_stay(turned, pieces, cots):
+    depth = pieces[0].shape[1]
+    half = cots[0].shape[1] // 2
+    return pl.pallas_call(
+        stay_kernel,
+        in_specs=[VMEM] * (1 + XS),
+        out_specs=VMEM,
+        out_shape=jax.ShapeDtypeStruct((depth, half), jnp.bfloat16),
+        cost_estimate=gradient_cost(pieces, cots),
+        name="stay",
+    )(turned, *cots)
+
+
+def backward_kernel(c0, c1, c2, c3, w0, w1, w2, w3, o0, o1, o2, o3):
+    alpha = R ** (-0.5)
+    cols = w0.shape[1]
+    for c, out in ((c0, o0), (c1, o1), (c2, o2), (c3, o3)):
+        total = None
+        for i, w in enumerate((w0, w1, w2, w3)):
+            part = lax.dot_general(
+                c[:, i * cols : (i + 1) * cols],
+                w[...],
+                (((1,), (1,)), ((), ())),
+                preferred_element_type=jnp.float32,
+            )
+            total = part if total is None else total + part
+        out[...] = (alpha * total).astype(jnp.bfloat16)
+
+
+def backward(pieces, blocks):
+    toks, rows = pieces[0].shape[0], blocks[0].shape[0]
+    return pl.pallas_call(
+        backward_kernel,
+        in_specs=[VMEM] * 8,
+        out_specs=[VMEM] * XS,
+        out_shape=[jax.ShapeDtypeStruct((toks, rows), jnp.bfloat16)] * XS,
+        cost_estimate=pl.CostEstimate(
+            flops=8 * pieces[0].size * rows,
+            bytes_accessed=8 * (pieces[0].size + blocks[0].size + toks * rows),
+            transcendentals=0,
+        ),
+        name="backward",
+    )(*pieces, *blocks)
 
 
 def body(saved_weight, saved_first, saved_second, saved_order, mask, hidden, cotangent):
     f32, bf16 = jnp.float32, jnp.bfloat16
     band = saved_order.shape[0]
-    toks, rows = hidden.shape
+    _, rows = hidden.shape
     cols = mask.shape[1]
     f = lax.axis_index("fsdp")
     t = lax.axis_index("tensor")
     zh, x, core = f >> 3, (f >> 1) & 3, f & 1
     zl, y = t >> 2, t & 3
-    alpha = R ** (-0.5)
 
     pick = (saved_order[None, :] == jnp.arange(band, dtype=jnp.int32)[:, None]).astype(bf16)
 
@@ -107,7 +227,7 @@
     pieces = [hidden]
     for k in (1, 2, 3):
         pieces.append(shift_x(hidden, k))
-    hidden_all = stacked(pieces)
+    hidden_pieces = pieces
 
     def cot_for(k):
         there = (x + k) & 3
@@ -129,24 +249,19 @@
     masked_zh = swap_zh(masked)
     masked_far = swap_core(masked_zh)
 
+    def token_block_at(yy):
+        e = (yy - x) & 3
+        there = jnp.where(e == 0, SPREAD[0], jnp.where(e == 2, SPREAD[2], e))
+        return (-there) & 3
+
+    order = jnp.stack([token_block_at((y + k) & 3) for k in range(YS)]).astype(jnp.int32)
+
     def output_half(own, other, near):
-        parts = []
-        for block in (own, other):
-            product = alpha * jnp.dot(hidden_all, block, preferred_element_type=f32)
-            parts.append(product.astype(bf16).reshape(XS, toks, cols))
-
-        def chunk_of(yy):
-            e = (yy - x) & 3
-            there = jnp.where(e == 0, SPREAD[0], jnp.where(e == 2, SPREAD[2], e))
-            k = (-there) & 3
-            return jnp.concatenate(
-                [lax.dynamic_index_in_dim(p, k, axis=0, keepdims=False) for p in parts], axis=1
-            )
-
+        chunks = forward(order, hidden_pieces, own, other)
+        own_chunk = chunks[0]
         got = []
         for k in (1, 2, 3):
-            got.append(shift_y(chunk_of((y + k) & 3), k))
-        own_chunk = chunk_of(y)
+            got.append(shift_y(chunks[k], k))
         total = own_chunk.astype(f32)
         for piece in got:
             total = total + piece.astype(f32)
@@ -162,12 +277,7 @@
     out_far = output_half(masked_zh, masked_far, False)
     output = jnp.where(zl == zh, out_near, out_far)
 
-    columns = jnp.concatenate([masked, masked_zh, masked_core, masked_far], axis=1)
-    cot_all = stacked(cot_pieces)
-    back = (
-        alpha
-        * lax.dot_general(cot_all, columns, (((1,), (1,)), ((), ())), preferred_element_type=f32)
-    ).astype(bf16).reshape(XS, toks, rows)
+    back = backward(cot_pieces, [masked, masked_zh, masked_core, masked_far])
     got = []
     for k in (1, 2, 3):
         got.append(shift_x(back[k], -k))
@@ -176,16 +286,8 @@
         hidden_grad = hidden_grad + piece.astype(f32)
     hidden_grad = hidden_grad.astype(bf16)
 
-    def product(block):
-        return (
-            alpha
-            * lax.dot_general(
-                hidden_all, block, (((0,), (0,)), ((), ())), preferred_element_type=f32
-            )
-        ).astype(bf16)
-
-    away = product(cot_all[:, 2 * cols :])
-    stay = product(cot_all[:, : 2 * cols])
+    away, turned = gradient_away(hidden_pieces, cot_pieces)
+    stay = gradient_stay(turned, hidden_pieces, cot_pieces)
     from_core = swap_core(away)
     far = (stay[:, cols:].astype(f32) + from_core[:, cols:].astype(f32)).astype(bf16)
     from_zh = swap_zh(far)

time: 245 us -> 277 us (1.13)
  the two profiles are of different devices: /device:TPU:1 before, /device:TPU:70 now
where the time goes in v1:
time: 277 us; the launch traced here: 276 us
  waiting for transfers between devices  139 us (50%)
  starting transfers between devices  60.2 us (22%)
  Pallas kernels  31.2 us (11%)
  other arithmetic  30.1 us (11%)
  local copies, waits for them, and re-layouts  11.8 us (4%)
    ppermute x9, waiting for transfers between devices, shift_x(): return lax.ppermute(value, 'fsdp', pairs)  52.9 us
    ppermute x2, waiting for transfers between devices, swap_zh(): return lax.ppermute(value, 'fsdp', [(i, i ^ 8) for i in range(16)])  33 us
    ppermute x6, waiting for transfers between devices, shift_y(): return lax.ppermute(value, 'tensor', pairs)  22.9 us
    all_to_all x2, starting transfers between devices, to_columns(): lax.all_to_all(blocks, 'fsdp', split_axis=0, concat_axis=0, tiled=True)  16.4 us
    ppermute x9, starting transfers between devices, shift_x(): return lax.ppermute(value, 'fsdp', pairs)  12 us
    ppermute x2, waiting for transfers between devices, swap_zl_half(): return lax.ppermute(value, ('fsdp', 'tensor'), pairs)  12 us
    all_to_all x2, starting transfers between devices, to_rows(): lax.all_to_all(blocks, 'tensor', split_axis=0, concat_axis=0, tiled=True)  11.1 us
    pallas_call x2, Pallas kernels, forward(): pl.pallas_call(forward_kernel, in_specs=[SMEM] + [VMEM] * (XS + 2), out_s...  10.5 us
  transfers between devices with their start and end apart: 28, of which 11 were waited for; matrix products, arithmetic and copies ran while one was open for 15% of the time, Pallas kernels for 11%

profile of v1, /device:TPU:70, one launch (start us, length us, event | category | flops | bytes accessed | tf_op | source)
XLA Modules:
  0.0 276.0 jit_solution(7867247292487262230)
XLA Ops:
  4.1 7.9 %all-to-all-start = ((bf16[16,56,512]{2,1,0:T(8,128)(2,1)}), bf16[16,56,512]{2,1,0:T(8,128)(2,1)}, u32[]{:S(2)}, u32[]{:S(2)}) async-start(bf16[16,56,512]{2,1,0:T(8,128)(2,1)} %bitcast.36), calls=%async_computation | async-start | bytes 1835008 | tf_op jit(solution)/shard_map/all_to_all | solution.py:216
  12.0 3.3 %constant_dynamic-slice_fusion.3 = (bf16[256,512]{1,0:T(8,128)(2,1)S(1)}, bf16[256,512]{1,0:T(8,128)(2,1)S(1)}, bf16[256,512]{1,0:T(8,128)(2,1)S(1)}, bf16[256,5...) fusion(bf16[256,8192]{1,0:T(8,128)(2,1)} %param.13, ...), kind=kLoop, calls=%fused_computation.44 | loop fusion | bytes 8388672 | tf_op jit(solution)/shard_map/dynamic_slice | solution.py:235
  24.5 5.5 %all-to-all-start.1 = ((bf16[16,56,512]{2,1,0:T(8,128)(2,1)}), bf16[16,56,512]{2,1,0:T(8,128)(2,1)S(1)}, u32[]{:S(2)}, u32[]{:S(2)}) async-start(bf16[16,56,512]{2,1,0:T(8,128)(2,1)} %all-to-all-done), calls=%async_computation.1 | async-start | bytes 1835008 | tf_op jit(solution)/shard_map/all_to_all | solution.py:220
  33.5 10.2 %all-to-all-done.1 = bf16[16,56,512]{2,1,0:T(8,128)(2,1)S(1)} async-done(((bf16[16,56,512]{2,1,0:T(8,128)(2,1)}), bf16[16,56,512]{2,1,0:T(8,128)(2,1)S(1)}, u32[]{:S(2)}, u32[]{:S(2)}) %all-to-all-start.1) | async-done | bytes 917536 | tf_op jit(solution)/shard_map/all_to_all | solution.py:220
  44.6 8.5 %all-to-all-start.2 = ((bf16[16,112,512]{2,1,0:T(8,128)(2,1)}), bf16[16,112,512]{2,1,0:T(8,128)(2,1)}, u32[]{:S(2)}, u32[]{:S(2)}) async-start(bf16[16,112,512]{2,1,0:T(8,128)(2,1)} %pad_maximum_fusion), calls=%async_computation.2 | async-start | bytes 3670016 | tf_op jit(solution)/shard_map/all_to_all | solution.py:216
  55.8 45.2 %collective-permute-done.1.h2 = bf16[256,896]{1,0:T(8,128)(2,1)S(1)} collective-permute-done((bf16[256,896]{1,0:T(8,128)(2,1)S(1)}, bf16[256,896]{1,0:T(8,128)(2,1)S(1)}, u32[]{:S(2)}, u32[]{:S(2)}) %collective-permute-start.1) | collective-permute-done | bytes 458784 | tf_op jit(solution)/shard_map/ppermute | solution.py:37
  101.0 7.7 %collective-permute-done.2.h3 = bf16[256,896]{1,0:T(8,128)(2,1)S(1)} collective-permute-done((bf16[256,896]{1,0:T(8,128)(2,1)S(1)}, bf16[256,896]{1,0:T(8,128)(2,1)S(1)}, u32[]{:S(2)}, u32[]{:S(2)}) %collective-permute-start.2) | collective-permute-done | bytes 458784 | tf_op jit(solution)/shard_map/ppermute | solution.py:37
  109.5 6.1 %away.1 = (bf16[896,1024]{1,0:T(8,128)(2,1)}, bf16[896,1024]{1,0:T(8,128)(2,1)}) custom-call(bf16[256,896]{1,0:T(8,128)(2,1)} %h0.5, bf16[256,896]{1,0:T(8,128)(2,1)} %collective-permute-done.h1, bf16[256,896]{1,0:T(8,128)(2,1)} %copy-done.13, bf16[256,896]{1,0:T(8,128)(2,1)} %copy-done.14, bf16[256,2048]{1,0:T(8,128)(2,1)} %pad_maximum_fusion.1.c0, ...), custom_call_target="tpu_custom_call" | custom-call | flops 1879048192 | bytes 5767168 | tf_op jit(solution)/shard_map/away/pallas_call | solution.py:141
  119.1 5.5 %all-to-all-start.3 = ((bf16[16,112,512]{2,1,0:T(8,128)(2,1)}), bf16[16,112,512]{2,1,0:T(8,128)(2,1)}, u32[]{:S(2)}, u32[]{:S(2)}) async-start(bf16[16,112,512]{2,1,0:T(8,128)(2,1)} %all-to-all-done.2), calls=%async_computation.3 | async-start | bytes 3670016 | tf_op jit(solution)/shard_map/all_to_all | solution.py:220
  125.3 33.0 %collective-permute-done.9.own.w1 = bf16[896,512]{1,0:T(8,128)(2,1)} collective-permute-done((bf16[896,512]{1,0:T(8,128)(2,1)}, bf16[896,512]{1,0:T(8,128)(2,1)}, u32[]{:S(2)}, u32[]{:S(2)}) %collective-permute-start.9) | collective-permute-done | bytes 917536 | tf_op jit(solution)/shard_map/ppermute | solution.py:41
  158.3 5.3 %forward.2 = (bf16[256,1024]{1,0:T(8,128)(2,1)}, bf16[256,1024]{1,0:T(8,128)(2,1)}, bf16[256,1024]{1,0:T(8,128)(2,1)}, bf16[256,1024]{1,0:T(8,128)(2,1)}) custom-call(s32[4]{0:T(128)} %pad_add_fusion.order, bf16[256,896]{1,0:T(8,128)(2,1)} %h0.5, bf16[256,896]{1,0:T(8,128)(2,1)} %collective-permute-done.h1, bf16[256,896]{1,0:T(8,128)(2,1)} %copy-done.13, ...), custom_call_target="tpu_custom_call" | custom-call | flops 1879048192 | bytes 5767168 | tf_op jit(solution)/shard_map/forward/pallas_call | solution.py:91
  168.2 6.0 %stay.1 = bf16[896,1024]{1,0:T(8,128)(2,1)} custom-call(bf16[896,1024]{1,0:T(8,128)(2,1)} %get-tuple-element.31.h_turned, bf16[256,2048]{1,0:T(8,128)(2,1)} %pad_maximum_fusion.1.c0, bf16[256,2048]{1,0:T(8,128)(2,1)} %collective-permute-done.16.c1, bf16[256,2048]{1,0:T(8,128)(2,1)} %collective-permute-done.17.c2, bf16[256,2048]{1,0:T(8,128)(2,1)} %collective-permute-done.18.c3), custom_call_target="tpu_custom_call" | custom-call | flops 1879048192 | bytes 5767168 | tf_op jit(solution)/shard_map/stay/pallas_call | solution.py:157
  177.5 12.5 %collective-permute-done.6 = bf16[256,1024]{1,0:T(8,128)(2,1)} collective-permute-done((bf16[256,1024]{1,0:T(8,128)(2,1)}, bf16[256,1024]{1,0:T(8,128)(2,1)}, u32[]{:S(2)}, u32[]{:S(2)}) %collective-permute-start.6) | collective-permute-done | bytes 524320 | tf_op jit(solution)/shard_map/ppermute | solution.py:50
  190.0 3.7 %collective-permute-done.4 = bf16[256,1024]{1,0:T(8,128)(2,1)} collective-permute-done((bf16[256,1024]{1,0:T(8,128)(2,1)}, bf16[256,1024]{1,0:T(8,128)(2,1)}, u32[]{:S(2)}, u32[]{:S(2)}) %collective-permute-start.4) | collective-permute-done | bytes 524320 | tf_op jit(solution)/shard_map/ppermute | solution.py:50
  196.2 4.3 %collective-permute-start.7 = (bf16[256,1024]{1,0:T(8,128)(2,1)}, bf16[256,1024]{1,0:T(8,128)(2,1)}, u32[]{:S(2)}, u32[]{:S(2)}) collective-permute-start(bf16[256,1024]{1,0:T(8,128)(2,1)} %fusion.7), channel_id=1, source_target_pairs={{4,0},{5,1},{6,2},{7,3},{12,8},{13,9},{14,10},{15,11},{20,16},{21,... | collective-permute-start | bytes 1572872 | tf_op jit(solution)/shard_map/ppermute | solution.py:59
  203.4 5.3 %forward.3 = (bf16[256,1024]{1,0:T(8,128)(2,1)}, bf16[256,1024]{1,0:T(8,128)(2,1)}, bf16[256,1024]{1,0:T(8,128)(2,1)}, bf16[256,1024]{1,0:T(8,128)(2,1)}) custom-call(s32[4]{0:T(128)} %pad_add_fusion.order, bf16[256,896]{1,0:T(8,128)(2,1)} %h0.5, bf16[256,896]{1,0:T(8,128)(2,1)} %collective-permute-done.h1, bf16[256,896]{1,0:T(8,128)(2,1)} %copy-done.13, ...), custom_call_target="tpu_custom_call" | custom-call | flops 1879048192 | bytes 5767168 | tf_op jit(solution)/shard_map/forward/pallas_call | solution.py:91
  210.7 3.9 %convert_multiply_fusion.2 = (f32[16,56,512]{2,1,0:T(8,128)}, f32[16,56,512]{2,1,0:T(8,128)}) fusion(bf16[16,112,512]{2,1,0:T(8,128)(2,1)} %bitcast.37), kind=kLoop, calls=%fused_computation.15 | loop fusion | flops 1835008 | bytes 5505024 | tf_op jit(solution)/shard_map/mul | solution.py:307
  214.6 8.6 %backward.1 = (bf16[256,896]{1,0:T(8,128)(2,1)}, bf16[256,896]{1,0:T(8,128)(2,1)}, bf16[256,896]{1,0:T(8,128)(2,1)}, bf16[256,896]{1,0:T(8,128)(2,1)}) custom-call(bf16[256,2048]{1,0:T(8,128)(2,1)} %pad_maximum_fusion.1.c0, bf16[256,2048]{1,0:T(8,128)(2,1)} %collective-permute-done.16.c1, bf16[256,2048]{1,0:T(8,128)(2,1)} %collective-permute-done.17.c2, ...), custom_call_target="tpu_custom_call" | custom-call | flops 3758096384 | bytes 9699328 | tf_op jit(solution)/shard_map/backward/pallas_call | solution.py:185
  226.0 3.4 %collective-permute-start.20 = (bf16[256,896]{1,0:T(8,128)(2,1)}, bf16[256,896]{1,0:T(8,128)(2,1)S(1)}, u32[]{:S(2)}, u32[]{:S(2)}) collective-permute-start(bf16[256,896]{1,0:T(8,128)(2,1)} %get-tuple-element.29), channel_id=1, source_target_pairs={{0,32},{8,40},{16,48},{24,56},{32,0},{40,8},{48,16},{56,24},{64,96... | collective-permute-start | bytes 1376264 | tf_op jit(solution)/shard_map/ppermute | solution.py:37
  229.3 6.0 %collective-permute-done.11 = bf16[256,1024]{1,0:T(8,128)(2,1)} collective-permute-done((bf16[256,1024]{1,0:T(8,128)(2,1)}, bf16[256,1024]{1,0:T(8,128)(2,1)}, u32[]{:S(2)}, u32[]{:S(2)}) %collective-permute-start.11) | collective-permute-done | bytes 524320 | tf_op jit(solution)/shard_map/ppermute | solution.py:50
  242.2 12.0 %collective-permute-done.14 = bf16[256,1024]{1,0:T(8,128)(2,1)S(1)} collective-permute-done((bf16[256,1024]{1,0:T(8,128)(2,1)S(1)}, bf16[256,1024]{1,0:T(8,128)(2,1)S(1)}, u32[]{:S(2)}, u32[]{:S(2)}) %collective-permute-start.14) | collective-permute-done | bytes 524320 | tf_op jit(solution)/shard_map/ppermute | solution.py:59
  257.1 6.6 %collective-permute-start.15 = (bf16[256,1024]{1,0:T(8,128)(2,1)S(1)}, bf16[256,1024]{1,0:T(8,128)(2,1)S(1)}, u32[]{:S(2)}, u32[]{:S(2)}) collective-permute-start(bf16[256,1024]{1,0:T(8,128)(2,1)S(1)} %maximum_select_fusion.1), channel_id=1, source_target_pairs={{4,36},{5,20},{6,4},{7,52},{12,44},{13,28},{14,12},{15,60},{20,5},... | collective-permute-start | bytes 1572872 | tf_op jit(solution)/shard_map/ppermute | solution.py:70
  263.7 5.3 %fusion.2 = (f32[896,512]{1,0:T(8,128)}, f32[896,512]{1,0:T(8,128)}, f32[896,512]{1,0:T(8,128)}) fusion(s32[896,512]{1,0:T(8,128)S(1)} %copy-done, bf16[2,8,56,512]{3,2,1,0:T(8,128)(2,1)S(1)} %copy.17, bf16[896,512]{1,0:T(8,128)(2,1)} %collective-permute-done.23, bf16[896,1024]{1,0:T(8,128)(2,1)} %collective-permute-done.22, ...), kind=kLoop, calls=%fused_computation.8 | loop fusion | flops 9633792 | bytes 14680064 | tf_op jit(solution)/shard_map/mul | solution.py:312
  270.0 5.1 %collective-permute-done.15 = bf16[256,1024]{1,0:T(8,128)(2,1)S(1)} collective-permute-done((bf16[256,1024]{1,0:T(8,128)(2,1)S(1)}, bf16[256,1024]{1,0:T(8,128)(2,1)S(1)}, u32[]{:S(2)}, u32[]{:S(2)}) %collective-permute-start.15) | collective-permute-done | bytes 524320 | tf_op jit(solution)/shard_map/ppermute | solution.py:70
  (95 shorter events, 54.3 us)
Async XLA Ops:
  0.6 54.0 %collective-permute-start = (bf16[256,896]{1,0:T(8,128)(2,1)}, bf16[256,896]{1,0:T(8,128)(2,1)}, u32[]{:S(2)}, u32[]{:S(2)}) collective-permute-start(bf16[256,896]{1,0:T(8,128)(2,1)} %h0.5), channel_id=1, source_target_pairs={{0,16},{8,24},{16,32},{24,40},{32,48},{40,56},{48,0},{56,8},{64,80... | collective-permute-start | bytes 1376264 | tf_op jit(solution)/shard_map/ppermute | solution.py:37
  4.1 20.4 %all-to-all-start = ((bf16[16,56,512]{2,1,0:T(8,128)(2,1)}), bf16[16,56,512]{2,1,0:T(8,128)(2,1)}, u32[]{:S(2)}, u32[]{:S(2)}) async-start(bf16[16,56,512]{2,1,0:T(8,128)(2,1)} %bitcast.36), calls=%async_computation | async-start | bytes 1835008 | tf_op jit(solution)/shard_map/all_to_all | solution.py:216
  16.4 92.3 %collective-permute-start.16 = (bf16[256,2048]{1,0:T(8,128)(2,1)}, bf16[256,2048]{1,0:T(8,128)(2,1)}, u32[]{:S(2)}, u32[]{:S(2)}) collective-permute-start(bf16[256,2048]{1,0:T(8,128)(2,1)} %pad_maximum_fusion.2), channel_id=1, source_target_pairs={{0,16},{8,24},{16,32},{24,40},{32,48},{40,56},{48,0},{56,8},{64,80... | collective-permute-start | bytes 3145736 | tf_op jit(solution)/shard_map/ppermute | solution.py:37
  18.1 90.7 %collective-permute-start.17 = (bf16[256,2048]{1,0:T(8,128)(2,1)}, bf16[256,2048]{1,0:T(8,128)(2,1)}, u32[]{:S(2)}, u32[]{:S(2)}) collective-permute-start(bf16[256,2048]{1,0:T(8,128)(2,1)} %pad_maximum_fusion.3), channel_id=1, source_target_pairs={{0,32},{8,40},{16,48},{24,56},{32,0},{40,8},{48,16},{56,24},{64,96... | collective-permute-start | bytes 3145736 | tf_op jit(solution)/shard_map/ppermute | solution.py:37
  21.6 87.2 %collective-permute-start.18 = (bf16[256,2048]{1,0:T(8,128)(2,1)}, bf16[256,2048]{1,0:T(8,128)(2,1)}, u32[]{:S(2)}, u32[]{:S(2)}) collective-permute-start(bf16[256,2048]{1,0:T(8,128)(2,1)} %pad_maximum_fusion.4), channel_id=1, source_target_pairs={{0,48},{8,56},{16,0},{24,8},{32,16},{40,24},{48,32},{56,40},{64,11... | collective-permute-start | bytes 3145736 | tf_op jit(solution)/shard_map/ppermute | solution.py:37
  24.5 19.2 %all-to-all-start.1 = ((bf16[16,56,512]{2,1,0:T(8,128)(2,1)}), bf16[16,56,512]{2,1,0:T(8,128)(2,1)S(1)}, u32[]{:S(2)}, u32[]{:S(2)}) async-start(bf16[16,56,512]{2,1,0:T(8,128)(2,1)} %all-to-all-done), calls=%async_computation.1 | async-start | bytes 1835008 | tf_op jit(solution)/shard_map/all_to_all | solution.py:220
  44.6 74.4 %all-to-all-start.2 = ((bf16[16,112,512]{2,1,0:T(8,128)(2,1)}), bf16[16,112,512]{2,1,0:T(8,128)(2,1)}, u32[]{:S(2)}, u32[]{:S(2)}) async-start(bf16[16,112,512]{2,1,0:T(8,128)(2,1)} %pad_maximum_fusion), calls=%async_computation.2 | async-start | bytes 3670016 | tf_op jit(solution)/shard_map/all_to_all | solution.py:216
  53.1 47.9 %collective-permute-start.1 = (bf16[256,896]{1,0:T(8,128)(2,1)S(1)}, bf16[256,896]{1,0:T(8,128)(2,1)S(1)}, u32[]{:S(2)}, u32[]{:S(2)}) collective-permute-start(bf16[256,896]{1,0:T(8,128)(2,1)S(1)} %copy-done.12), channel_id=1, source_target_pairs={{0,32},{8,40},{16,48},{24,56},{32,0},{40,8},{48,16},{56,24},{64,96... | collective-permute-start | bytes 1376264 | tf_op jit(solution)/shard_map/ppermute | solution.py:37
  54.6 54.1 %collective-permute-start.2 = (bf16[256,896]{1,0:T(8,128)(2,1)S(1)}, bf16[256,896]{1,0:T(8,128)(2,1)S(1)}, u32[]{:S(2)}, u32[]{:S(2)}) collective-permute-start(bf16[256,896]{1,0:T(8,128)(2,1)S(1)} %copy-done.12), channel_id=1, source_target_pairs={{0,48},{8,56},{16,0},{24,8},{32,16},{40,24},{48,32},{56,40},{64,11... | collective-permute-start | bytes 1376264 | tf_op jit(solution)/shard_map/ppermute | solution.py:37
  115.5 58.7 %collective-permute-start.22 = (bf16[896,1024]{1,0:T(8,128)(2,1)}, bf16[896,1024]{1,0:T(8,128)(2,1)}, u32[]{:S(2)}, u32[]{:S(2)}) collective-permute-start(bf16[896,1024]{1,0:T(8,128)(2,1)} %get-tuple-element.32), channel_id=1, source_target_pairs={{0,8},{8,0},{16,24},{24,16},{32,40},{40,32},{48,56},{56,48},{64,72... | collective-permute-start | bytes 5505032 | tf_op jit(solution)/shard_map/ppermute | solution.py:45
  118.5 39.8 %collective-permute-start.9 = (bf16[896,512]{1,0:T(8,128)(2,1)}, bf16[896,512]{1,0:T(8,128)(2,1)}, u32[]{:S(2)}, u32[]{:S(2)}) collective-permute-start(bf16[896,512]{1,0:T(8,128)(2,1)} %bitcast_multiply_fusion.own.w0), channel_id=1, source_target_pairs={{0,64},{8,72},{16,80},{24,88},{32,96},{40,104},{48,112},{56,120},{... | collective-permute-start | bytes 2752520 | tf_op jit(solution)/shard_map/ppermute | solution.py:41
  119.1 39.2 %collective-permute-start.3 = (bf16[896,512]{1,0:T(8,128)(2,1)}, bf16[896,512]{1,0:T(8,128)(2,1)}, u32[]{:S(2)}, u32[]{:S(2)}) collective-permute-start(bf16[896,512]{1,0:T(8,128)(2,1)} %bitcast_multiply_fusion.own.w0), channel_id=1, source_target_pairs={{0,8},{8,0},{16,24},{24,16},{32,40},{40,32},{48,56},{56,48},{64,72... | collective-permute-start | bytes 2752520 | tf_op jit(solution)/shard_map/ppermute | solution.py:45
  119.1 81.5 %all-to-all-start.3 = ((bf16[16,112,512]{2,1,0:T(8,128)(2,1)}), bf16[16,112,512]{2,1,0:T(8,128)(2,1)}, u32[]{:S(2)}, u32[]{:S(2)}) async-start(bf16[16,112,512]{2,1,0:T(8,128)(2,1)} %all-to-all-done.2), calls=%async_computation.3 | async-start | bytes 3670016 | tf_op jit(solution)/shard_map/all_to_all | solution.py:220
  158.3 45.1 %collective-permute-start.10 = (bf16[896,512]{1,0:T(8,128)(2,1)}, bf16[896,512]{1,0:T(8,128)(2,1)}, u32[]{:S(2)}, u32[]{:S(2)}) collective-permute-start(bf16[896,512]{1,0:T(8,128)(2,1)} %collective-permute-done.9.own.w1), channel_id=1, source_target_pairs={{0,8},{8,0},{16,24},{24,16},{32,40},{40,32},{48,56},{56,48},{64,72... | collective-permute-start | bytes 2752520 | tf_op jit(solution)/shard_map/ppermute | solution.py:45
  163.6 26.4 %collective-permute-start.6 = (bf16[256,1024]{1,0:T(8,128)(2,1)}, bf16[256,1024]{1,0:T(8,128)(2,1)}, u32[]{:S(2)}, u32[]{:S(2)}) collective-permute-start(bf16[256,1024]{1,0:T(8,128)(2,1)} %get-tuple-element.22), channel_id=1, source_target_pairs={{0,3},{1,0},{2,1},{3,2},{4,7},{5,4},{6,5},{7,6},{8,11},{9,8},{10,9... | collective-permute-start | bytes 1572872 | tf_op jit(solution)/shard_map/ppermute | solution.py:50
  166.6 23.4 %collective-permute-start.5 = (bf16[256,1024]{1,0:T(8,128)(2,1)}, bf16[256,1024]{1,0:T(8,128)(2,1)}, u32[]{:S(2)}, u32[]{:S(2)}) collective-permute-start(bf16[256,1024]{1,0:T(8,128)(2,1)} %get-tuple-element.21), channel_id=1, source_target_pairs={{0,2},{1,3},{2,0},{3,1},{4,6},{5,7},{6,4},{7,5},{8,10},{9,11},{10,... | collective-permute-start | bytes 1572872 | tf_op jit(solution)/shard_map/ppermute | solution.py:50
  167.2 26.5 %collective-permute-start.4 = (bf16[256,1024]{1,0:T(8,128)(2,1)}, bf16[256,1024]{1,0:T(8,128)(2,1)}, u32[]{:S(2)}, u32[]{:S(2)}) collective-permute-start(bf16[256,1024]{1,0:T(8,128)(2,1)} %get-tuple-element.20), channel_id=1, source_target_pairs={{0,1},{1,2},{2,3},{3,0},{4,5},{5,6},{6,7},{7,4},{8,9},{9,10},{10,1... | collective-permute-start | bytes 1572872 | tf_op jit(solution)/shard_map/ppermute | solution.py:50
  176.9 80.2 %collective-permute-start.23 = (bf16[896,512]{1,0:T(8,128)(2,1)}, bf16[896,512]{1,0:T(8,128)(2,1)}, u32[]{:S(2)}, u32[]{:S(2)}) collective-permute-start(bf16[896,512]{1,0:T(8,128)(2,1)} %add_convert_fusion), channel_id=1, source_target_pairs={{0,64},{8,72},{16,80},{24,88},{32,96},{40,104},{48,112},{56,120},{... | collective-permute-start | bytes 2752520 | tf_op jit(solution)/shard_map/ppermute | solution.py:41
  196.2 42.5 %collective-permute-start.7 = (bf16[256,1024]{1,0:T(8,128)(2,1)}, bf16[256,1024]{1,0:T(8,128)(2,1)}, u32[]{:S(2)}, u32[]{:S(2)}) collective-permute-start(bf16[256,1024]{1,0:T(8,128)(2,1)} %fusion.7), channel_id=1, source_target_pairs={{4,0},{5,1},{6,2},{7,3},{12,8},{13,9},{14,10},{15,11},{20,16},{21,... | collective-permute-start | bytes 1572872 | tf_op jit(solution)/shard_map/ppermute | solution.py:59
  209.9 25.4 %collective-permute-start.11 = (bf16[256,1024]{1,0:T(8,128)(2,1)}, bf16[256,1024]{1,0:T(8,128)(2,1)}, u32[]{:S(2)}, u32[]{:S(2)}) collective-permute-start(bf16[256,1024]{1,0:T(8,128)(2,1)} %get-tuple-element.24), channel_id=1, source_target_pairs={{0,1},{1,2},{2,3},{3,0},{4,5},{5,6},{6,7},{7,4},{8,9},{9,10},{10,1... | collective-permute-start | bytes 1572872 | tf_op jit(solution)/shard_map/ppermute | solution.py:50
  223.8 45.2 %collective-permute-start.21 = (bf16[256,896]{1,0:T(8,128)(2,1)}, bf16[256,896]{1,0:T(8,128)(2,1)S(1)}, u32[]{:S(2)}, u32[]{:S(2)}) collective-permute-start(bf16[256,896]{1,0:T(8,128)(2,1)} %get-tuple-element.30), channel_id=1, source_target_pairs={{0,16},{8,24},{16,32},{24,40},{32,48},{40,56},{48,0},{56,8},{64,80... | collective-permute-start | bytes 1376264 | tf_op jit(solution)/shard_map/ppermute | solution.py:37
  226.0 43.0 %collective-permute-start.20 = (bf16[256,896]{1,0:T(8,128)(2,1)}, bf16[256,896]{1,0:T(8,128)(2,1)S(1)}, u32[]{:S(2)}, u32[]{:S(2)}) collective-permute-start(bf16[256,896]{1,0:T(8,128)(2,1)} %get-tuple-element.29), channel_id=1, source_target_pairs={{0,32},{8,40},{16,48},{24,56},{32,0},{40,8},{48,16},{56,24},{64,96... | collective-permute-start | bytes 1376264 | tf_op jit(solution)/shard_map/ppermute | solution.py:37
  235.3 33.7 %collective-permute-start.19 = (bf16[256,896]{1,0:T(8,128)(2,1)}, bf16[256,896]{1,0:T(8,128)(2,1)S(1)}, u32[]{:S(2)}, u32[]{:S(2)}) collective-permute-start(bf16[256,896]{1,0:T(8,128)(2,1)} %get-tuple-element.28), channel_id=1, source_target_pairs={{0,48},{8,56},{16,0},{24,8},{32,16},{40,24},{48,32},{56,40},{64,11... | collective-permute-start | bytes 1376264 | tf_op jit(solution)/shard_map/ppermute | solution.py:37
  257.1 18.1 %collective-permute-start.15 = (bf16[256,1024]{1,0:T(8,128)(2,1)S(1)}, bf16[256,1024]{1,0:T(8,128)(2,1)S(1)}, u32[]{:S(2)}, u32[]{:S(2)}) collective-permute-start(bf16[256,1024]{1,0:T(8,128)(2,1)S(1)} %maximum_select_fusion.1), channel_id=1, source_target_pairs={{4,36},{5,20},{6,4},{7,52},{12,44},{13,28},{14,12},{15,60},{20,5},... | collective-permute-start | bytes 1572872 | tf_op jit(solution)/shard_map/ppermute | solution.py:70
  (19 other events, 197.9 us)

commit v2 on v1

--- a/solution.py
+++ b/solution.py
@@ -101,6 +101,26 @@
         ),
         name="forward",
     )(order, *pieces, own, other)
+
+
+def joined_kernel(at, q0, q1, q2, q3, out):
+    part = q0.shape[0]
+    for k, piece in enumerate((q0, q1, q2, q3)):
+        out[pl.ds(pl.multiple_of(at[k] * part, part), part), :] = piece[...]
+
+
+def joined(at, pieces):
+    part, width = pieces[0].shape
+    return pl.pallas_call(
+        joined_kernel,
+        in_specs=[SMEM] + [VMEM] * YS,
+        out_specs=VMEM,
+        out_shape=jax.ShapeDtypeStruct((YS * part, width), pieces[0].dtype),
+        cost_estimate=pl.CostEstimate(
+            flops=0, bytes_accessed=4 * YS * part * width, transcendentals=0
+        ),
+        name="joined",
+    )(at, *pieces)
 
 
 def turned_product(h_turned, c_refs, lo, hi):
@@ -199,7 +219,7 @@
 def body(saved_weight, saved_first, saved_second, saved_order, mask, hidden, cotangent):
     f32, bf16 = jnp.float32, jnp.bfloat16
     band = saved_order.shape[0]
-    _, rows = hidden.shape
+    toks, rows = hidden.shape
     cols = mask.shape[1]
     f = lax.axis_index("fsdp")
     t = lax.axis_index("tensor")
@@ -229,20 +249,28 @@
         pieces.append(shift_x(hidden, k))
     hidden_pieces = pieces
 
-    def cot_for(k):
+    def cot_for(k, first_row, n):
         there = (x + k) & 3
         parts = [
-            lax.dynamic_slice_in_dim(
-                cotangent, fsdp_id(zh ^ zr, there, core ^ cr) * cols, cols, axis=1
+            lax.dynamic_slice(
+                cotangent, (first_row, fsdp_id(zh ^ zr, there, core ^ cr) * cols), (n, cols)
             )
             for cr in (0, 1)
             for zr in (0, 1)
         ]
         return jnp.concatenate(parts, axis=1)
 
-    pieces = [cot_for(0)]
+    part = toks // YS
+    quarter = shift_x(cot_for(2, y * part, part), 2)
+    pieces = [cot_for(0, 0, toks)]
+    pieces.append(shift_x(cot_for(1, 0, toks), 1))
+    last = shift_x(cot_for(3, 0, toks), 3)
+    quarters = [quarter]
     for k in (1, 2, 3):
-        pieces.append(shift_x(cot_for(k), k))
+        quarters.append(shift_y(quarter, k))
+    at = jnp.stack([(y - k) & 3 for k in range(YS)]).astype(jnp.int32)
+    pieces.append(joined(at, quarters))
+    pieces.append(last)
     cot_pieces = pieces
 
     masked_core = swap_core(masked)

time: 277 us -> 261 us (0.942)
  the two profiles are of different devices: /device:TPU:70 before, /device:TPU:38 now
where the time goes in v2:
time: 261 us
  waiting for transfers between devices  111 us (43%)
  starting transfers between devices  69.4 us (27%)
  Pallas kernels  33.4 us (13%)
  other arithmetic  31.4 us (12%)
  local copies, waits for them, and re-layouts  11.9 us (5%)
  matrix products  2.68 us (1%)
    ppermute x2, waiting for transfers between devices, swap_zh(): return lax.ppermute(value, 'fsdp', [(i, i ^ 8) for i in range(16)])  30.4 us
    ppermute x9, waiting for transfers between devices, shift_y(): return lax.ppermute(value, 'tensor', pairs)  30.1 us
    ppermute x9, waiting for transfers between devices, shift_x(): return lax.ppermute(value, 'fsdp', pairs)  18.4 us
    ppermute x9, starting transfers between devices, shift_x(): return lax.ppermute(value, 'fsdp', pairs)  18.1 us
    all_to_all x2, starting transfers between devices, to_columns(): lax.all_to_all(blocks, 'fsdp', split_axis=0, concat_axis=0, tiled=True)  13.7 us
    ppermute x2, waiting for transfers between devices, swap_zl_half(): return lax.ppermute(value, ('fsdp', 'tensor'), pairs)  12 us
    all_to_all x2, starting transfers between devices, to_rows(): lax.all_to_all(blocks, 'tensor', split_axis=0, concat_axis=0, tiled=True)  11.7 us
    pallas_call x2, Pallas kernels, forward(): pl.pallas_call(forward_kernel, in_specs=[SMEM] + [VMEM] * (XS + 2), out_s...  10.5 us
  transfers between devices with their start and end apart: 31, of which 13 were waited for; matrix products, arithmetic and copies ran while one was open for 15% of the time, Pallas kernels for 13%

profile of v2, /device:TPU:38, one launch (start us, length us, event | category | flops | bytes accessed | tf_op | source)
XLA Modules:
  0.0 260.5 jit_solution(14544225777419964543)
XLA Ops:
  3.5 7.2 %all-to-all-start = ((bf16[16,56,512]{2,1,0:T(8,128)(2,1)}), bf16[16,56,512]{2,1,0:T(8,128)(2,1)}, u32[]{:S(2)}, u32[]{:S(2)}) async-start(bf16[16,56,512]{2,1,0:T(8,128)(2,1)} %bitcast.40), calls=%async_computation | async-start | bytes 1835008 | tf_op jit(solution)/shard_map/all_to_all | solution.py:236
  24.0 5.9 %all-to-all-start.1 = ((bf16[16,56,512]{2,1,0:T(8,128)(2,1)}), bf16[16,56,512]{2,1,0:T(8,128)(2,1)S(1)}, u32[]{:S(2)}, u32[]{:S(2)}) async-start(bf16[16,56,512]{2,1,0:T(8,128)(2,1)} %all-to-all-done), calls=%async_computation.1 | async-start | bytes 1835008 | tf_op jit(solution)/shard_map/all_to_all | solution.py:240
  33.4 10.4 %all-to-all-done.1 = bf16[16,56,512]{2,1,0:T(8,128)(2,1)S(1)} async-done(((bf16[16,56,512]{2,1,0:T(8,128)(2,1)}), bf16[16,56,512]{2,1,0:T(8,128)(2,1)S(1)}, u32[]{:S(2)}, u32[]{:S(2)}) %all-to-all-start.1) | async-done | bytes 917536 | tf_op jit(solution)/shard_map/all_to_all | solution.py:240
  44.7 6.5 %all-to-all-start.2 = ((bf16[16,112,512]{2,1,0:T(8,128)(2,1)}), bf16[16,112,512]{2,1,0:T(8,128)(2,1)}, u32[]{:S(2)}, u32[]{:S(2)}) async-start(bf16[16,112,512]{2,1,0:T(8,128)(2,1)} %pad_maximum_fusion), calls=%async_computation.2 | async-start | bytes 3670016 | tf_op jit(solution)/shard_map/all_to_all | solution.py:236
  54.9 11.8 %collective-permute-done.18.q1 = bf16[64,2048]{1,0:T(8,128)(2,1)S(1)} collective-permute-done((bf16[64,2048]{1,0:T(8,128)(2,1)}, bf16[64,2048]{1,0:T(8,128)(2,1)S(1)}, u32[]{:S(2)}, u32[]{:S(2)}) %collective-permute-start.18) | collective-permute-done | bytes 262176 | tf_op jit(solution)/shard_map/ppermute | solution.py:50
  74.4 9.1 %collective-permute-done.h1 = bf16[256,896]{1,0:T(8,128)(2,1)S(1)} collective-permute-done((bf16[256,896]{1,0:T(8,128)(2,1)S(1)}, bf16[256,896]{1,0:T(8,128)(2,1)S(1)}, u32[]{:S(2)}, u32[]{:S(2)}) %collective-permute-start) | collective-permute-done | bytes 458784 | tf_op jit(solution)/shard_map/ppermute | solution.py:37
  85.7 7.2 %collective-permute-done.2.h3 = bf16[256,896]{1,0:T(8,128)(2,1)} collective-permute-done((bf16[256,896]{1,0:T(8,128)(2,1)S(1)}, bf16[256,896]{1,0:T(8,128)(2,1)}, u32[]{:S(2)}, u32[]{:S(2)}) %collective-permute-start.2) | collective-permute-done | bytes 458784 | tf_op jit(solution)/shard_map/ppermute | solution.py:37
  92.9 6.1 %away.1 = (bf16[896,1024]{1,0:T(8,128)(2,1)}, bf16[896,1024]{1,0:T(8,128)(2,1)}) custom-call(bf16[256,896]{1,0:T(8,128)(2,1)} %h0.5, bf16[256,896]{1,0:T(8,128)(2,1)} %copy-done.16, bf16[256,896]{1,0:T(8,128)(2,1)} %copy-done.17, bf16[256,896]{1,0:T(8,128)(2,1)} %collective-permute-done.2.h3, bf16[256,2048]{1,0:T(8,128)(2,1)} %pad_maximum_fusion.1.c0, ...), custom_call_target="tpu_custom_call" | custom-call | flops 1879048192 | bytes 5767168 | tf_op jit(solution)/shard_map/away/pallas_call | solution.py:161
  104.7 5.8 %all-to-all-start.3 = ((bf16[16,112,512]{2,1,0:T(8,128)(2,1)}), bf16[16,112,512]{2,1,0:T(8,128)(2,1)}, u32[]{:S(2)}, u32[]{:S(2)}) async-start(bf16[16,112,512]{2,1,0:T(8,128)(2,1)} %all-to-all-done.2), calls=%async_computation.3 | async-start | bytes 3670016 | tf_op jit(solution)/shard_map/all_to_all | solution.py:240
  111.2 30.4 %collective-permute-done.9.own.w1 = bf16[896,512]{1,0:T(8,128)(2,1)} collective-permute-done((bf16[896,512]{1,0:T(8,128)(2,1)}, bf16[896,512]{1,0:T(8,128)(2,1)}, u32[]{:S(2)}, u32[]{:S(2)}) %collective-permute-start.9) | collective-permute-done | bytes 917536 | tf_op jit(solution)/shard_map/ppermute | solution.py:41
  141.6 5.3 %forward.2 = (bf16[256,1024]{1,0:T(8,128)(2,1)}, bf16[256,1024]{1,0:T(8,128)(2,1)}, bf16[256,1024]{1,0:T(8,128)(2,1)}, bf16[256,1024]{1,0:T(8,128)(2,1)}) custom-call(s32[4]{0:T(128)} %pad_add_fusion.order, bf16[256,896]{1,0:T(8,128)(2,1)} %h0.5, bf16[256,896]{1,0:T(8,128)(2,1)} %copy-done.16, bf16[256,896]{1,0:T(8,128)(2,1)} %copy-done.17, ...), custom_call_target="tpu_custom_call" | custom-call | flops 1879048192 | bytes 5767168 | tf_op jit(solution)/shard_map/forward/pallas_call | solution.py:91
  149.8 6.0 %stay.1 = bf16[896,1024]{1,0:T(8,128)(2,1)} custom-call(bf16[896,1024]{1,0:T(8,128)(2,1)} %get-tuple-element.31.h_turned, bf16[256,2048]{1,0:T(8,128)(2,1)} %pad_maximum_fusion.1.c0, bf16[256,2048]{1,0:T(8,128)(2,1)} %collective-permute-done.16.c1, bf16[256,2048]{1,0:T(8,128)(2,1)} %joined.1.c2, bf16[256,2048]{1,0:T(8,128)(2,1)} %collective-permute-done.21.c3), custom_call_target="tpu_custom_call" | custom-call | flops 1879048192 | bytes 5767168 | tf_op jit(solution)/shard_map/stay/pallas_call | solution.py:177
  165.1 10.5 %collective-permute-done.4 = bf16[256,1024]{1,0:T(8,128)(2,1)} collective-permute-done((bf16[256,1024]{1,0:T(8,128)(2,1)}, bf16[256,1024]{1,0:T(8,128)(2,1)}, u32[]{:S(2)}, u32[]{:S(2)}) %collective-permute-start.4) | collective-permute-done | bytes 524320 | tf_op jit(solution)/shard_map/ppermute | solution.py:50
  178.0 3.8 %collective-permute-start.7 = (bf16[256,1024]{1,0:T(8,128)(2,1)}, bf16[256,1024]{1,0:T(8,128)(2,1)}, u32[]{:S(2)}, u32[]{:S(2)}) collective-permute-start(bf16[256,1024]{1,0:T(8,128)(2,1)} %fusion.7), channel_id=1, source_target_pairs={{4,0},{5,1},{6,2},{7,3},{12,8},{13,9},{14,10},{15,11},{20,16},{21,... | collective-permute-start | bytes 1572872 | tf_op jit(solution)/shard_map/ppermute | solution.py:59
  184.8 5.3 %forward.3 = (bf16[256,1024]{1,0:T(8,128)(2,1)}, bf16[256,1024]{1,0:T(8,128)(2,1)}, bf16[256,1024]{1,0:T(8,128)(2,1)}, bf16[256,1024]{1,0:T(8,128)(2,1)}) custom-call(s32[4]{0:T(128)} %pad_add_fusion.order, bf16[256,896]{1,0:T(8,128)(2,1)} %h0.5, bf16[256,896]{1,0:T(8,128)(2,1)} %copy-done.16, bf16[256,896]{1,0:T(8,128)(2,1)} %copy-done.17, ...), custom_call_target="tpu_custom_call" | custom-call | flops 1879048192 | bytes 5767168 | tf_op jit(solution)/shard_map/forward/pallas_call | solution.py:91
  193.2 3.8 %convert_multiply_fusion.2 = (f32[16,56,512]{2,1,0:T(8,128)}, f32[16,56,512]{2,1,0:T(8,128)}) fusion(bf16[16,112,512]{2,1,0:T(8,128)(2,1)} %bitcast.41), kind=kLoop, calls=%fused_computation.15 | loop fusion | flops 1835008 | bytes 5505024 | tf_op jit(solution)/shard_map/mul | solution.py:335
  197.0 8.5 %backward.1 = (bf16[256,896]{1,0:T(8,128)(2,1)}, bf16[256,896]{1,0:T(8,128)(2,1)}, bf16[256,896]{1,0:T(8,128)(2,1)}, bf16[256,896]{1,0:T(8,128)(2,1)}) custom-call(bf16[256,2048]{1,0:T(8,128)(2,1)} %pad_maximum_fusion.1.c0, bf16[256,2048]{1,0:T(8,128)(2,1)} %collective-permute-done.16.c1, bf16[256,2048]{1,0:T(8,128)(2,1)} %joined.1.c2, ...), custom_call_target="tpu_custom_call" | custom-call | flops 3758096384 | bytes 9699328 | tf_op jit(solution)/shard_map/backward/pallas_call | solution.py:205
  205.6 3.4 %collective-permute-start.24 = (bf16[256,896]{1,0:T(8,128)(2,1)}, bf16[256,896]{1,0:T(8,128)(2,1)S(1)}, u32[]{:S(2)}, u32[]{:S(2)}) collective-permute-start(bf16[256,896]{1,0:T(8,128)(2,1)} %get-tuple-element.30), channel_id=1, source_target_pairs={{0,16},{8,24},{16,32},{24,40},{32,48},{40,56},{48,0},{56,8},{64,80... | collective-permute-start | bytes 1376264 | tf_op jit(solution)/shard_map/ppermute | solution.py:37
  212.3 4.3 %collective-permute-done.11 = bf16[256,1024]{1,0:T(8,128)(2,1)} collective-permute-done((bf16[256,1024]{1,0:T(8,128)(2,1)}, bf16[256,1024]{1,0:T(8,128)(2,1)}, u32[]{:S(2)}, u32[]{:S(2)}) %collective-permute-start.11) | collective-permute-done | bytes 524320 | tf_op jit(solution)/shard_map/ppermute | solution.py:50
  216.6 4.7 %collective-permute-start.22 = (bf16[256,896]{1,0:T(8,128)(2,1)}, bf16[256,896]{1,0:T(8,128)(2,1)S(1)}, u32[]{:S(2)}, u32[]{:S(2)}) collective-permute-start(bf16[256,896]{1,0:T(8,128)(2,1)} %get-tuple-element.28), channel_id=1, source_target_pairs={{0,48},{8,56},{16,0},{24,8},{32,16},{40,24},{48,32},{56,40},{64,11... | collective-permute-start | bytes 1376264 | tf_op jit(solution)/shard_map/ppermute | solution.py:37
  226.7 12.0 %collective-permute-done.14 = bf16[256,1024]{1,0:T(8,128)(2,1)S(1)} collective-permute-done((bf16[256,1024]{1,0:T(8,128)(2,1)S(1)}, bf16[256,1024]{1,0:T(8,128)(2,1)S(1)}, u32[]{:S(2)}, u32[]{:S(2)}) %collective-permute-start.14) | collective-permute-done | bytes 524320 | tf_op jit(solution)/shard_map/ppermute | solution.py:59
  241.6 4.4 %collective-permute-start.15 = (bf16[256,1024]{1,0:T(8,128)(2,1)S(1)}, bf16[256,1024]{1,0:T(8,128)(2,1)S(1)}, u32[]{:S(2)}, u32[]{:S(2)}) collective-permute-start(bf16[256,1024]{1,0:T(8,128)(2,1)S(1)} %maximum_select_fusion.1), channel_id=1, source_target_pairs={{4,36},{5,20},{6,4},{7,52},{12,44},{13,28},{14,12},{15,60},{20,5},... | collective-permute-start | bytes 1572872 | tf_op jit(solution)/shard_map/ppermute | solution.py:70
  246.1 5.3 %fusion.2 = (f32[896,512]{1,0:T(8,128)}, f32[896,512]{1,0:T(8,128)}, f32[896,512]{1,0:T(8,128)}) fusion(s32[896,512]{1,0:T(8,128)S(1)} %copy-done, bf16[2,8,56,512]{3,2,1,0:T(8,128)(2,1)S(1)} %copy.17, bf16[896,512]{1,0:T(8,128)(2,1)} %collective-permute-done.26, bf16[896,1024]{1,0:T(8,128)(2,1)} %collective-permute-done.25, ...), kind=kLoop, calls=%fused_computation.8 | loop fusion | flops 9633792 | bytes 14680064 | tf_op jit(solution)/shard_map/mul | solution.py:340
  252.4 7.3 %collective-permute-done.15 = bf16[256,1024]{1,0:T(8,128)(2,1)S(1)} collective-permute-done((bf16[256,1024]{1,0:T(8,128)(2,1)S(1)}, bf16[256,1024]{1,0:T(8,128)(2,1)S(1)}, u32[]{:S(2)}, u32[]{:S(2)}) %collective-permute-start.15) | collective-permute-done | bytes 524320 | tf_op jit(solution)/shard_map/ppermute | solution.py:70
  (110 shorter events, 74.8 us)
Async XLA Ops:
  3.5 20.5 %all-to-all-start = ((bf16[16,56,512]{2,1,0:T(8,128)(2,1)}), bf16[16,56,512]{2,1,0:T(8,128)(2,1)}, u32[]{:S(2)}, u32[]{:S(2)}) async-start(bf16[16,56,512]{2,1,0:T(8,128)(2,1)} %bitcast.40), calls=%async_computation | async-start | bytes 1835008 | tf_op jit(solution)/shard_map/all_to_all | solution.py:236
  14.8 78.0 %collective-permute-start.16 = (bf16[256,2048]{1,0:T(8,128)(2,1)}, bf16[256,2048]{1,0:T(8,128)(2,1)}, u32[]{:S(2)}, u32[]{:S(2)}) collective-permute-start(bf16[256,2048]{1,0:T(8,128)(2,1)} %pad_maximum_fusion.2), channel_id=1, source_target_pairs={{0,16},{8,24},{16,32},{24,40},{32,48},{40,56},{48,0},{56,8},{64,80... | collective-permute-start | bytes 3145736 | tf_op jit(solution)/shard_map/ppermute | solution.py:37
  16.8 34.5 %collective-permute-start.17 = (bf16[64,2048]{1,0:T(8,128)(2,1)}, bf16[64,2048]{1,0:T(8,128)(2,1)}, u32[]{:S(2)}, u32[]{:S(2)}) collective-permute-start(bf16[64,2048]{1,0:T(8,128)(2,1)} %pad_maximum_fusion.4), channel_id=1, source_target_pairs={{0,32},{8,40},{16,48},{24,56},{32,0},{40,8},{48,16},{56,24},{64,96... | collective-permute-start | bytes 786440 | tf_op jit(solution)/shard_map/ppermute | solution.py:37
  21.6 71.2 %collective-permute-start.21 = (bf16[256,2048]{1,0:T(8,128)(2,1)}, bf16[256,2048]{1,0:T(8,128)(2,1)}, u32[]{:S(2)}, u32[]{:S(2)}) collective-permute-start(bf16[256,2048]{1,0:T(8,128)(2,1)} %pad_maximum_fusion.3), channel_id=1, source_target_pairs={{0,48},{8,56},{16,0},{24,8},{32,16},{40,24},{48,32},{56,40},{64,11... | collective-permute-start | bytes 3145736 | tf_op jit(solution)/shard_map/ppermute | solution.py:37
  24.0 19.7 %all-to-all-start.1 = ((bf16[16,56,512]{2,1,0:T(8,128)(2,1)}), bf16[16,56,512]{2,1,0:T(8,128)(2,1)S(1)}, u32[]{:S(2)}, u32[]{:S(2)}) async-start(bf16[16,56,512]{2,1,0:T(8,128)(2,1)} %all-to-all-done), calls=%async_computation.1 | async-start | bytes 1835008 | tf_op jit(solution)/shard_map/all_to_all | solution.py:240
  44.7 60.0 %all-to-all-start.2 = ((bf16[16,112,512]{2,1,0:T(8,128)(2,1)}), bf16[16,112,512]{2,1,0:T(8,128)(2,1)}, u32[]{:S(2)}, u32[]{:S(2)}) async-start(bf16[16,112,512]{2,1,0:T(8,128)(2,1)} %pad_maximum_fusion), calls=%async_computation.2 | async-start | bytes 3670016 | tf_op jit(solution)/shard_map/all_to_all | solution.py:236
  66.7 16.8 %collective-permute-start = (bf16[256,896]{1,0:T(8,128)(2,1)S(1)}, bf16[256,896]{1,0:T(8,128)(2,1)S(1)}, u32[]{:S(2)}, u32[]{:S(2)}) collective-permute-start(bf16[256,896]{1,0:T(8,128)(2,1)S(1)} %copy-done.15), channel_id=1, source_target_pairs={{0,16},{8,24},{16,32},{24,40},{32,48},{40,56},{48,0},{56,8},{64,80... | collective-permute-start | bytes 1376264 | tf_op jit(solution)/shard_map/ppermute | solution.py:37
  66.7 19.0 %collective-permute-start.1 = (bf16[256,896]{1,0:T(8,128)(2,1)S(1)}, bf16[256,896]{1,0:T(8,128)(2,1)S(1)}, u32[]{:S(2)}, u32[]{:S(2)}) collective-permute-start(bf16[256,896]{1,0:T(8,128)(2,1)S(1)} %copy-done.15), channel_id=1, source_target_pairs={{0,32},{8,40},{16,48},{24,56},{32,0},{40,8},{48,16},{56,24},{64,96... | collective-permute-start | bytes 1376264 | tf_op jit(solution)/shard_map/ppermute | solution.py:37
  68.2 24.6 %collective-permute-start.2 = (bf16[256,896]{1,0:T(8,128)(2,1)S(1)}, bf16[256,896]{1,0:T(8,128)(2,1)}, u32[]{:S(2)}, u32[]{:S(2)}) collective-permute-start(bf16[256,896]{1,0:T(8,128)(2,1)S(1)} %copy-done.15), channel_id=1, source_target_pairs={{0,48},{8,56},{16,0},{24,8},{32,16},{40,24},{48,32},{56,40},{64,11... | collective-permute-start | bytes 1376264 | tf_op jit(solution)/shard_map/ppermute | solution.py:37
  98.9 56.9 %collective-permute-start.25 = (bf16[896,1024]{1,0:T(8,128)(2,1)}, bf16[896,1024]{1,0:T(8,128)(2,1)}, u32[]{:S(2)}, u32[]{:S(2)}) collective-permute-start(bf16[896,1024]{1,0:T(8,128)(2,1)} %get-tuple-element.32), channel_id=1, source_target_pairs={{0,8},{8,0},{16,24},{24,16},{32,40},{40,32},{48,56},{56,48},{64,72... | collective-permute-start | bytes 5505032 | tf_op jit(solution)/shard_map/ppermute | solution.py:45
  101.8 39.8 %collective-permute-start.9 = (bf16[896,512]{1,0:T(8,128)(2,1)}, bf16[896,512]{1,0:T(8,128)(2,1)}, u32[]{:S(2)}, u32[]{:S(2)}) collective-permute-start(bf16[896,512]{1,0:T(8,128)(2,1)} %bitcast_multiply_fusion.own.w0), channel_id=1, source_target_pairs={{0,64},{8,72},{16,80},{24,88},{32,96},{40,104},{48,112},{56,120},{... | collective-permute-start | bytes 2752520 | tf_op jit(solution)/shard_map/ppermute | solution.py:41
  104.7 36.9 %collective-permute-start.3 = (bf16[896,512]{1,0:T(8,128)(2,1)}, bf16[896,512]{1,0:T(8,128)(2,1)}, u32[]{:S(2)}, u32[]{:S(2)}) collective-permute-start(bf16[896,512]{1,0:T(8,128)(2,1)} %bitcast_multiply_fusion.own.w0), channel_id=1, source_target_pairs={{0,8},{8,0},{16,24},{24,16},{32,40},{40,32},{48,56},{56,48},{64,72... | collective-permute-start | bytes 2752520 | tf_op jit(solution)/shard_map/ppermute | solution.py:45
  104.7 77.1 %all-to-all-start.3 = ((bf16[16,112,512]{2,1,0:T(8,128)(2,1)}), bf16[16,112,512]{2,1,0:T(8,128)(2,1)}, u32[]{:S(2)}, u32[]{:S(2)}) async-start(bf16[16,112,512]{2,1,0:T(8,128)(2,1)} %all-to-all-done.2), calls=%async_computation.3 | async-start | bytes 3670016 | tf_op jit(solution)/shard_map/all_to_all | solution.py:240
  141.6 43.1 %collective-permute-start.10 = (bf16[896,512]{1,0:T(8,128)(2,1)}, bf16[896,512]{1,0:T(8,128)(2,1)}, u32[]{:S(2)}, u32[]{:S(2)}) collective-permute-start(bf16[896,512]{1,0:T(8,128)(2,1)} %collective-permute-done.9.own.w1), channel_id=1, source_target_pairs={{0,8},{8,0},{16,24},{24,16},{32,40},{40,32},{48,56},{56,48},{64,72... | collective-permute-start | bytes 2752520 | tf_op jit(solution)/shard_map/ppermute | solution.py:45
  148.4 16.7 %collective-permute-start.5 = (bf16[256,1024]{1,0:T(8,128)(2,1)}, bf16[256,1024]{1,0:T(8,128)(2,1)}, u32[]{:S(2)}, u32[]{:S(2)}) collective-permute-start(bf16[256,1024]{1,0:T(8,128)(2,1)} %get-tuple-element.21), channel_id=1, source_target_pairs={{0,2},{1,3},{2,0},{3,1},{4,6},{5,7},{6,4},{7,5},{8,10},{9,11},{10,... | collective-permute-start | bytes 1572872 | tf_op jit(solution)/shard_map/ppermute | solution.py:50
  149.8 25.7 %collective-permute-start.4 = (bf16[256,1024]{1,0:T(8,128)(2,1)}, bf16[256,1024]{1,0:T(8,128)(2,1)}, u32[]{:S(2)}, u32[]{:S(2)}) collective-permute-start(bf16[256,1024]{1,0:T(8,128)(2,1)} %get-tuple-element.20), channel_id=1, source_target_pairs={{0,1},{1,2},{2,3},{3,0},{4,5},{5,6},{6,7},{7,4},{8,9},{9,10},{10,1... | collective-permute-start | bytes 1572872 | tf_op jit(solution)/shard_map/ppermute | solution.py:50
  158.5 83.1 %collective-permute-start.26 = (bf16[896,512]{1,0:T(8,128)(2,1)}, bf16[896,512]{1,0:T(8,128)(2,1)}, u32[]{:S(2)}, u32[]{:S(2)}) collective-permute-start(bf16[896,512]{1,0:T(8,128)(2,1)} %add_convert_fusion), channel_id=1, source_target_pairs={{0,64},{8,72},{16,80},{24,88},{32,96},{40,104},{48,112},{56,120},{... | collective-permute-start | bytes 2752520 | tf_op jit(solution)/shard_map/ppermute | solution.py:41
  178.0 45.2 %collective-permute-start.7 = (bf16[256,1024]{1,0:T(8,128)(2,1)}, bf16[256,1024]{1,0:T(8,128)(2,1)}, u32[]{:S(2)}, u32[]{:S(2)}) collective-permute-start(bf16[256,1024]{1,0:T(8,128)(2,1)} %fusion.7), channel_id=1, source_target_pairs={{4,0},{5,1},{6,2},{7,3},{12,8},{13,9},{14,10},{15,11},{20,16},{21,... | collective-permute-start | bytes 1572872 | tf_op jit(solution)/shard_map/ppermute | solution.py:59
  190.6 18.3 %collective-permute-start.12 = (bf16[256,1024]{1,0:T(8,128)(2,1)}, bf16[256,1024]{1,0:T(8,128)(2,1)}, u32[]{:S(2)}, u32[]{:S(2)}) collective-permute-start(bf16[256,1024]{1,0:T(8,128)(2,1)} %get-tuple-element.25), channel_id=1, source_target_pairs={{0,2},{1,3},{2,0},{3,1},{4,6},{5,7},{6,4},{7,5},{8,10},{9,11},{10,... | collective-permute-start | bytes 1572872 | tf_op jit(solution)/shard_map/ppermute | solution.py:50
  192.6 24.0 %collective-permute-start.11 = (bf16[256,1024]{1,0:T(8,128)(2,1)}, bf16[256,1024]{1,0:T(8,128)(2,1)}, u32[]{:S(2)}, u32[]{:S(2)}) collective-permute-start(bf16[256,1024]{1,0:T(8,128)(2,1)} %get-tuple-element.24), channel_id=1, source_target_pairs={{0,1},{1,2},{2,3},{3,0},{4,5},{5,6},{6,7},{7,4},{8,9},{9,10},{10,1... | collective-permute-start | bytes 1572872 | tf_op jit(solution)/shard_map/ppermute | solution.py:50
  205.6 45.8 %collective-permute-start.24 = (bf16[256,896]{1,0:T(8,128)(2,1)}, bf16[256,896]{1,0:T(8,128)(2,1)S(1)}, u32[]{:S(2)}, u32[]{:S(2)}) collective-permute-start(bf16[256,896]{1,0:T(8,128)(2,1)} %get-tuple-element.30), channel_id=1, source_target_pairs={{0,16},{8,24},{16,32},{24,40},{32,48},{40,56},{48,0},{56,8},{64,80... | collective-permute-start | bytes 1376264 | tf_op jit(solution)/shard_map/ppermute | solution.py:37
  209.0 42.4 %collective-permute-start.23 = (bf16[256,896]{1,0:T(8,128)(2,1)}, bf16[256,896]{1,0:T(8,128)(2,1)S(1)}, u32[]{:S(2)}, u32[]{:S(2)}) collective-permute-start(bf16[256,896]{1,0:T(8,128)(2,1)} %get-tuple-element.29), channel_id=1, source_target_pairs={{0,32},{8,40},{16,48},{24,56},{32,0},{40,8},{48,16},{56,24},{64,96... | collective-permute-start | bytes 1376264 | tf_op jit(solution)/shard_map/ppermute | solution.py:37
  216.6 34.8 %collective-permute-start.22 = (bf16[256,896]{1,0:T(8,128)(2,1)}, bf16[256,896]{1,0:T(8,128)(2,1)S(1)}, u32[]{:S(2)}, u32[]{:S(2)}) collective-permute-start(bf16[256,896]{1,0:T(8,128)(2,1)} %get-tuple-element.28), channel_id=1, source_target_pairs={{0,48},{8,56},{16,0},{24,8},{32,16},{40,24},{48,32},{56,40},{64,11... | collective-permute-start | bytes 1376264 | tf_op jit(solution)/shard_map/ppermute | solution.py:37
  241.6 18.1 %collective-permute-start.15 = (bf16[256,1024]{1,0:T(8,128)(2,1)S(1)}, bf16[256,1024]{1,0:T(8,128)(2,1)S(1)}, u32[]{:S(2)}, u32[]{:S(2)}) collective-permute-start(bf16[256,1024]{1,0:T(8,128)(2,1)S(1)} %maximum_select_fusion.1), channel_id=1, source_target_pairs={{4,36},{5,20},{6,4},{7,52},{12,44},{13,28},{14,12},{15,60},{20,5},... | collective-permute-start | bytes 1572872 | tf_op jit(solution)/shard_map/ppermute | solution.py:70
  (25 other events, 287.4 us)
